TPU v7x, 32 devices: a whole 2x2x4 slice. The times are simulated.
32 devices in a mesh: fsdp: 8 (over y, x, core), tp: 4 (over z).
Axes of the slice: x: 2, y: 2, z: 4, core: 2. Of those that a mesh axis runs over, the one named last changes fastest.
Arguments:
- tokens: bfloat16 [2, 2048, 2048], P(None, 'fsdp', 'tp'), may hold values from -6 to 6
- out_grad: bfloat16 [2, 2048, 2048], P(None, 'fsdp', 'tp'), may hold values from -6 to 6
- segment_ids: int32 [2, 2048], P(None, 'fsdp'), may hold values from 0 to 3, as said below
- positions: int32 [2, 2048], P(None, 'fsdp'), may hold values from 0 to 1023, as said below
- attn_norm: bfloat16 [2048], P('fsdp'), may hold values from 0.25 to 1.75
- w_query: bfloat16 [2048, 2048], P('fsdp', 'tp'), may hold values from -0.125 to 0.125
- key_projection_weight: bfloat16 [2048, 256], P('fsdp', 'tp'), may hold values from -0.125 to 0.125
- value_projection_weight: bfloat16 [2048, 256], P('fsdp', 'tp'), may hold values from -0.125 to 0.125
- w_out: bfloat16 [2048, 2048], P('tp', 'fsdp'), may hold values from -1 to 1
- mlp_norm: bfloat16 [2048], P('fsdp'), may hold values from 0.25 to 1.75
- w_gate: bfloat16 [2048, 5632], P('fsdp', 'tp'), may hold values from -0.125 to 0.125
- w_up: bfloat16 [2048, 5632], P('fsdp', 'tp'), may hold values from -0.125 to 0.125
- w_down: bfloat16 [5632, 2048], P('tp', 'fsdp'), may hold values from -0.078125 to 0.078125
Outputs:
- layer_out: bfloat16 [2, 2048, 2048], P(None, 'fsdp', 'tp')
- input_grad: float32 [2, 2048, 2048], P(None, 'fsdp', 'tp')
- grad_attn_norm: float32 [2048], P('fsdp')
- grad_query: float32 [2048, 2048], P('fsdp', 'tp')
- grad_key: float32 [2048, 256], P('fsdp', 'tp')
- grad_value: float32 [2048, 256], P('fsdp', 'tp')
- grad_out: float32 [2048, 2048], P('tp', 'fsdp')
- grad_mlp_norm: float32 [2048], P('fsdp')
- grad_gate: float32 [2048, 5632], P('fsdp', 'tp')
- grad_up: float32 [2048, 5632], P('fsdp', 'tp')
- grad_down: float32 [5632, 2048], P('tp', 'fsdp')
Inputs may be any that keep to these rules, and one draw needn't show every extreme that they name: `segment_ids`: within each sequence of 2048 tokens, taken in its own order, the ids run 0, 1, 2, 3 in order, each a contiguous run of 1 token or more; one run in each sequence is exactly 1024 tokens long. `positions`: each token's offset, in its sequence's order, from the first token of its run of equal segment_ids.
All inputs are finite; a program needn't handle non-finite values.
Results may differ from a plain program's by a relative error of at most 0.014.
Values may be sent and summed in bfloat16 or wider, within the bound.
No kernel may reach another device: no remote copies, remote signals or barrier semaphores. Data moves between devices by JAX's collectives and lax.ppermute only.
A program may use at most 256 MiB of HBM per device.

v0:
```python
import jax
import jax.numpy as jnp
from jax import lax
from jax.sharding import PartitionSpec as P


HEAD_SIZE = 64
SEQUENCE_LENGTH = 2048
DOC_MAX = 1024


NORM_EPSILON = 1e-05
ROPE_BASE = 10000.0
MASKED_SCORE = -1e30
GAIN_COLUMNS = 128

F32 = jnp.float32
BF16 = jnp.bfloat16


def rope_tables(offsets, head_width):
    half_width = head_width // 2
    inverse = ROPE_BASE ** (-(jnp.arange(half_width, dtype=F32) * 2.0 / head_width))
    angles = offsets.astype(F32)[:, None] * inverse[None, :]
    cosine_table = jnp.concatenate([jnp.cos(angles), jnp.cos(angles)], -1)
    sine_lookup = jnp.concatenate([jnp.sin(angles), jnp.sin(angles)], -1)
    return (cosine_table, sine_lookup)


def apply_rotary(vectors, cosine_table, sine_lookup):
    half_width = vectors.shape[-1] // 2
    turned = jnp.concatenate([-vectors[..., half_width:], vectors[..., :half_width]], -1)
    return vectors * cosine_table[:, None, :] + turned * sine_lookup[:, None, :]


def reverse_rotary(cotangent, cosine_table, sine_lookup):
    half_width = cotangent.shape[-1] // 2
    scaled = cotangent * sine_lookup[:, None, :]
    return cotangent * cosine_table[:, None, :] + jnp.concatenate(
        [scaled[..., half_width:], -scaled[..., :half_width]], -1
    )


def dot_nn(left, right):
    return jnp.dot(left, right, preferred_element_type=F32)


def dot_nt(left, right):
    return lax.dot_general(left, right, (((1,), (1,)), ((), ())), preferred_element_type=F32)


def dot_tn(left, right):
    return lax.dot_general(left, right, (((0,), (0,)), ((), ())), preferred_element_type=F32)


def exchange(block, axis, mask):
    return lax.ppermute(block, axis, [(i, i ^ mask) for i in range(lax.axis_size(axis))])


def passed_along(block, axis, distance):
    devices = range(lax.axis_size(axis))
    route = [(i - distance, i) for i in devices if i - distance in devices]
    return lax.ppermute(block, axis, route)


def tp_gather(part, *earlier):
    size = lax.axis_size("tp")
    index = lax.axis_index("tp")
    up, down = [part], [part]
    for step in range(1, size):
        lower, upper = up[-1], down[-1]
        if earlier and step == 2:
            lower, upper = after(lower, *earlier), after(upper, *earlier)
        up.append(lax.ppermute(lower, "tp", [(i, i + 1) for i in range(step - 1, size - 1)]))
        down.append(lax.ppermute(upper, "tp", [(i, i - 1) for i in range(1, size - step + 1)]))
    slots = []
    for slot in range(size):
        block = part
        for other in range(size):
            if other != slot:
                held = up[other - slot] if other > slot else down[slot - other]
                block = jnp.where(index == other, held, block)
        slots.append(block)
    return jnp.concatenate(slots, 1)


def tp_scatter_sum(partial):
    size = lax.axis_size("tp")
    index = lax.axis_index("tp")
    width = partial.shape[1] // size

    def slot(at):
        at = jnp.clip(at, 0, size - 1)
        return lax.dynamic_slice_in_dim(partial, at * width, width, 1)

    total = slot(index)
    lower = upper = None
    for step in range(1, size):
        to_upper, to_lower = slot(index + size - step), slot(index - size + step)
        if lower is not None:
            to_upper, to_lower = to_upper + lower.astype(F32), to_lower + upper.astype(F32)
        lower = lax.ppermute(
            to_upper.astype(BF16), "tp", [(i, i + 1) for i in range(min(step, size - 1))]
        )
        upper = lax.ppermute(
            to_lower.astype(BF16), "tp", [(i, i - 1) for i in range(size - step, size)]
        )
    return total + lower.astype(F32) + upper.astype(F32)


def queue_gather(part):
    return lax.all_gather(part, "tp", axis=1, tiled=True)


def queue_scatter_sum(partial):
    return lax.psum_scatter(partial.astype(BF16), "tp", scatter_dimension=1, tiled=True)


def owner_order(array):
    size = lax.axis_size("fsdp")
    index = lax.axis_index("fsdp")
    width = array.shape[1] // size
    cut = lambda owner: lax.dynamic_slice_in_dim(array, owner * width, width, 1)
    away = jnp.concatenate([cut(index ^ 1 ^ (2 * m)) for m in range(size // 2)], 1)
    return lax.optimization_barrier([away] + [cut(index ^ (2 * m)) for m in range(size // 2)])


def owner_terms(blocks, terms_of, axis):
    away = terms_of(blocks[0]).astype(BF16)
    other = exchange(away, "fsdp", 1)
    width = away.shape[axis] // (len(blocks) - 1)
    terms, sent = [], []
    for m, block in enumerate(blocks[1:]):
        share = lax.slice_in_dim(other, m * width, (m + 1) * width, axis=axis)
        term = terms_of(block) + share.astype(F32)
        if m:
            sent.append(term.astype(BF16))
        if m:
            term = exchange(sent[-1], "fsdp", 2 * m)
        terms.append(term)
    return terms, sent


def owner_total(terms, *earlier):
    terms = lax.optimization_barrier(tuple(terms) + earlier)[: len(terms)]
    return sum(term.astype(F32) for term in terms)


def after(value, *earlier):
    return lax.optimization_barrier((value,) + earlier)[0]


def allowed_keys(offsets, row_count, back):
    row = jnp.arange(row_count, dtype=jnp.int32)[:, None] + back * row_count
    first = row - offsets[..., None]
    key = jnp.arange((back + 1) * row_count, dtype=jnp.int32)[None, :]
    return ((key >= first) & (key <= row))[:, None]


def attend_forward(query_rotated, keys, values, allowed, score_scale):
    scores = (
        jnp.einsum("blhd,bmd->bhlm", query_rotated, keys, preferred_element_type=F32)
        * score_scale
    )
    scores = jnp.where(allowed, scores, MASKED_SCORE)
    row_max = jnp.max(scores, -1)
    row_sum = jnp.sum(jnp.where(allowed, jnp.exp(scores - row_max[..., None]), 0.0), -1)
    log_total = row_max + jnp.log(row_sum)
    prob_round = jnp.where(allowed, jnp.exp(scores - log_total[..., None]), 0.0).astype(BF16)
    heads = jnp.einsum("bhlm,bmd->blhd", prob_round, values, preferred_element_type=F32)
    return (heads.astype(BF16), log_total)


def attend_backward(
    query_rotated, keys, values, allowed, log_total, heads_low, grad_low, score_scale
):
    delta = jnp.swapaxes(jnp.sum(grad_low.astype(F32) * heads_low.astype(F32), -1), 1, 2)
    scores = (
        jnp.einsum("blhd,bmd->bhlm", query_rotated, keys, preferred_element_type=F32)
        * score_scale
    )
    prob_exact = jnp.where(allowed, jnp.exp(scores - log_total[..., None]), 0.0)
    prob_round = prob_exact.astype(BF16)
    grad_values = jnp.einsum("bhlm,blhd->bmd", prob_round, grad_low, preferred_element_type=F32)
    grad_probs = jnp.einsum("blhd,bmd->bhlm", grad_low, values, preferred_element_type=F32)
    grad_scores = (prob_exact * (grad_probs - delta[..., None]) * score_scale).astype(BF16)
    grad_query = jnp.einsum("bhlm,bmd->blhd", grad_scores, keys, preferred_element_type=F32)
    grad_keys = jnp.einsum(
        "bhlm,blhd->bmd", grad_scores, query_rotated, preferred_element_type=F32
    )
    return (grad_query, grad_keys, grad_values)


def shards(
    tokens,
    out_grad,
    segment_ids,
    positions,
    attn_norm,
    w_query,
    key_projection_weight,
    value_projection_weight,
    w_out,
    mlp_norm,
    w_gate,
    w_up,
    w_down,
):
    batch_count, row_count, local_width = tokens.shape
    full_width = local_width * lax.axis_size("tp")
    group_size = SEQUENCE_LENGTH // row_count
    stride = lax.axis_size("fsdp") // group_size
    query_width = w_query.shape[1]
    hidden = w_gate.shape[1]
    head_count = query_width // HEAD_SIZE
    score_scale = HEAD_SIZE ** (-0.5)
    back = min(group_size - 1, -(-(DOC_MAX - 1) // row_count))
    column_start = lax.axis_index("tp") * local_width

    gains = jnp.stack([attn_norm, mlp_norm], 1)
    gains = jnp.pad(gains, ((0, 0), (0, GAIN_COLUMNS - 2)))
    first_shard = jnp.concatenate(
        [w_query, key_projection_weight, value_projection_weight, gains], 1
    )
    project_width = query_width + 2 * HEAD_SIZE
    first_full = lax.all_gather(first_shard, "fsdp", axis=0, tiled=True)
    project_weight = first_full[:, :project_width]
    gain_rows = first_full[:, project_width : project_width + 2].astype(F32).T
    gain_one, gain_two = gain_rows[0], gain_rows[1]
    rows = batch_count * row_count
    tokens_own = tokens.reshape(rows, local_width)
    tokens_full = tp_gather(tokens_own)
    out_weight = lax.all_gather(after(w_out, tokens_full), "fsdp", axis=1, tiled=True)
    gate_up_shard = lax.optimization_barrier(jnp.concatenate([w_gate, w_up], 1))
    gate_up_weight = lax.all_gather(
        after(gate_up_shard, tokens_full), "fsdp", axis=0, tiled=True
    )
    down_weight = lax.all_gather(after(w_down, tokens_full), "fsdp", axis=1, tiled=True)

    by_batch = lambda array: array.reshape((batch_count, row_count) + array.shape[1:])
    all_rows = lambda array: array.reshape((rows,) + array.shape[2:])
    inputs = tokens_full.astype(F32)
    scale_one = lax.rsqrt(jnp.mean(inputs * inputs, -1, keepdims=True) + NORM_EPSILON)
    normed_one = (inputs * scale_one * gain_one).astype(BF16)
    projected = dot_nn(normed_one, project_weight)
    tables = rope_tables(positions.reshape(rows), HEAD_SIZE)
    allowed = allowed_keys(positions, row_count, back)
    query_rotated = by_batch(
        apply_rotary(
            projected[:, :query_width].reshape(rows, head_count, HEAD_SIZE), *tables
        ).astype(BF16)
    )
    key_rotated = apply_rotary(
        projected[:, None, query_width : query_width + HEAD_SIZE], *tables
    )[:, 0].astype(BF16)
    pairs = by_batch(
        jnp.concatenate([key_rotated, projected[:, query_width + HEAD_SIZE :].astype(BF16)], -1)
    )
    grad_in = tp_gather(after(out_grad.reshape(rows, local_width), tokens_full), pairs)
    window = [passed_along(pairs, "fsdp", o * stride) for o in range(back, 0, -1)]
    window = jnp.concatenate(window + [pairs], 1)
    keys, values = window[..., :HEAD_SIZE], window[..., HEAD_SIZE:]
    heads, totals = attend_forward(query_rotated, keys, values, allowed, score_scale)
    heads_out = heads.reshape(rows, query_width)
    middle_own = tokens_own.astype(F32) + tp_scatter_sum(
        dot_nn(after(heads_out, grad_in), out_weight)
    )
    middle = tp_gather(middle_own.astype(BF16)).astype(F32)

    scale_two = lax.rsqrt(jnp.mean(middle * middle, -1, keepdims=True) + NORM_EPSILON)
    normed_two = lax.optimization_barrier((middle * scale_two * gain_two).astype(BF16))
    both = dot_nn(normed_two, gate_up_weight)
    gate, up_proj = both[:, :hidden], both[:, hidden:]
    sigmoid_gate = jax.nn.sigmoid(gate)
    activated = (gate * sigmoid_gate * up_proj).astype(BF16)
    grad_act = dot_nn(grad_in, down_weight.T)
    grad_gate_low = (
        grad_act * up_proj * sigmoid_gate * (1.0 + gate * (1.0 - sigmoid_gate))
    ).astype(BF16)
    grad_up_low = (grad_act * gate * sigmoid_gate).astype(BF16)
    partial_two = queue_scatter_sum(
        dot_nt(grad_gate_low, gate_up_weight[:, :hidden])
        + dot_nt(grad_up_low, gate_up_weight[:, hidden:])
    )
    normed_two_order = owner_order(normed_two)
    gate_terms, gate_sent = owner_terms(
        normed_two_order, lambda block: dot_tn(block, grad_gate_low), 0
    )
    up_terms, up_sent = owner_terms(normed_two_order, lambda block: dot_tn(block, grad_up_low), 0)
    grads_order = owner_order(grad_in)
    down_terms, _ = owner_terms(grads_order, lambda block: dot_tn(activated, block), 1)
    grad_normed_two = queue_gather(after(partial_two, *gate_sent, *up_sent))
    mlp_own = queue_scatter_sum(after(dot_nn(activated, down_weight).astype(BF16), grad_normed_two))
    output = (middle_own + mlp_own.astype(F32)).astype(BF16)

    gain_one_own = lax.dynamic_slice_in_dim(gain_one, column_start, local_width, 0)
    grad_two = grad_normed_two.astype(F32)
    norm_sum_two = jnp.sum(grad_two * middle * scale_two, 0)
    scaled_two = grad_two * gain_two
    grad_middle = (
        grad_in.astype(F32)
        + scale_two * scaled_two
        - middle
        * (scale_two * scale_two * scale_two)
        * jnp.mean(scaled_two * middle, -1, keepdims=True)
    )
    middle_low = lax.optimization_barrier(grad_middle.astype(BF16))
    grad_heads = by_batch(
        dot_nt(middle_low, out_weight).astype(BF16).reshape(rows, head_count, HEAD_SIZE)
    )
    grad_query_rot, grad_keys, grad_values = attend_backward(
        query_rotated, keys, values, allowed, totals, heads, grad_heads, score_scale
    )
    grad_window = jnp.concatenate([grad_keys, grad_values], -1)
    own_pairs = grad_window[:, back * row_count :]
    for o in range(1, back + 1):
        block = grad_window[:, (back - o) * row_count : (back - o + 1) * row_count]
        own_pairs = own_pairs + passed_along(block.astype(BF16), "fsdp", -o * stride).astype(F32)
    own_pairs = all_rows(own_pairs)
    grad_query_low = (
        reverse_rotary(all_rows(grad_query_rot), *tables).reshape(rows, query_width).astype(BF16)
    )
    grad_key_low = reverse_rotary(own_pairs[:, None, :HEAD_SIZE], *tables)[:, 0].astype(BF16)
    grad_value_low = own_pairs[:, HEAD_SIZE:].astype(BF16)
    grad_projected = lax.optimization_barrier(
        jnp.concatenate([grad_query_low, grad_key_low, grad_value_low], 1)
    )
    grad_one = dot_nt(grad_projected, project_weight)
    weighted = grad_one * inputs
    norm_sum_one = jnp.sum(weighted * scale_one, 0)
    summed = queue_scatter_sum(after(grad_one.astype(BF16), mlp_own))
    small = jnp.concatenate([norm_sum_one, jnp.sum(weighted * gain_one, -1) / full_width])
    for bit in range((lax.axis_size("tp") - 1).bit_length()):
        small = small + exchange(small, "tp", 1 << bit)
    norm_sum_one, row_mean = small[:full_width], small[full_width:, None]
    grad_middle_own = lax.dynamic_slice_in_dim(grad_middle, column_start, local_width, 1)
    input_grad = (
        grad_middle_own
        + scale_one * (summed.astype(F32) * gain_one_own)
        - tokens_own.astype(F32) * (scale_one * scale_one * scale_one) * row_mean
    )
    middle_order = owner_order(middle_low)
    out_terms, _ = owner_terms(middle_order, lambda block: dot_tn(heads_out, block), 1)
    norm_order = owner_order(jnp.stack([norm_sum_one, norm_sum_two]))
    normed_one_order = owner_order(normed_one)
    project_terms, project_sent = owner_terms(
        list(zip(normed_one_order, norm_order)),
        lambda pair: jnp.concatenate(
            [
                dot_tn(pair[0], grad_projected),
                jnp.pad(pair[1].T, ((0, 0), (0, GAIN_COLUMNS - 2))),
            ],
            1,
        ),
        0,
    )
    grad_scale = (batch_count * row_count * lax.axis_size("fsdp")) ** (-0.5)
    down_sum = owner_total(down_terms, *project_sent)
    gate_sum = owner_total(gate_terms, *project_sent)
    up_sum = owner_total(up_terms, *project_sent)
    out_sum = owner_total(out_terms, *project_sent)
    project_sum = owner_total(project_terms) * grad_scale
    return (
        by_batch(output),
        by_batch(input_grad),
        project_sum[:, project_width],
        project_sum[:, :query_width],
        project_sum[:, query_width : query_width + HEAD_SIZE],
        project_sum[:, query_width + HEAD_SIZE : project_width],
        out_sum * grad_scale,
        project_sum[:, project_width + 1],
        gate_sum * grad_scale,
        up_sum * grad_scale,
        down_sum * grad_scale,
    )


def solution(mesh):
    in_specs = (
        P(None, "fsdp", "tp"),
        P(None, "fsdp", "tp"),
        P(None, "fsdp"),
        P(None, "fsdp"),
        P("fsdp"),
        P("fsdp", "tp"),
        P("fsdp", "tp"),
        P("fsdp", "tp"),
        P("tp", "fsdp"),
        P("fsdp"),
        P("fsdp", "tp"),
        P("fsdp", "tp"),
        P("tp", "fsdp"),
    )
    out_specs = (
        P(None, "fsdp", "tp"),
        P(None, "fsdp", "tp"),
        P("fsdp"),
        P("fsdp", "tp"),
        P("fsdp", "tp"),
        P("fsdp", "tp"),
        P("tp", "fsdp"),
        P("fsdp"),
        P("fsdp", "tp"),
        P("fsdp", "tp"),
        P("tp", "fsdp"),
    )

    return jax.shard_map(shards, mesh=mesh, in_specs=in_specs, out_specs=out_specs, check_vma=False)
```

profile of v0, /device:TPU:0, one launch (start us, length us, event | category | flops | bytes accessed | tf_op | source)
XLA Modules:
  0.0 567.5 jit_solution(7101448216883799268)
XLA Ops:
  18.6 10.1 %collective-permute-done = bf16[512,512]{1,0:T(8,128)(2,1)S(1)} collective-permute-done((bf16[512,512]{1,0:T(8,128)(2,1)}, bf16[512,512]{1,0:T(8,128)(2,1)S(1)}, u32[]{:S(2)}, u32[]{:S(2)}) %collective-permute-start) | collective-permute-done | bytes 524320 | tf_op jit(solution)/shard_map/ppermute | solution.py:74
  34.8 12.6 %collective-permute-done.4 = bf16[512,512]{1,0:T(8,128)(2,1)S(1)} collective-permute-done((bf16[512,512]{1,0:T(8,128)(2,1)S(1)}, bf16[512,512]{1,0:T(8,128)(2,1)S(1)}, u32[]{:S(2)}, u32[]{:S(2)}) %collective-permute-start.4) | collective-permute-done | bytes 524320 | tf_op jit(solution)/shard_map/ppermute | solution.py:75
  48.8 12.7 %collective-permute-done.5 = bf16[512,512]{1,0:T(8,128)(2,1)} collective-permute-done((bf16[512,512]{1,0:T(8,128)(2,1)S(1)}, bf16[512,512]{1,0:T(8,128)(2,1)}, u32[]{:S(2)}, u32[]{:S(2)}) %collective-permute-start.5) | collective-permute-done | bytes 524320 | tf_op jit(solution)/shard_map/ppermute | solution.py:75
  124.0 7.6 %collective-permute-done.15 = bf16[512,512]{1,0:T(8,128)(2,1)S(1)} collective-permute-done((bf16[512,512]{1,0:T(8,128)(2,1)S(1)}, bf16[512,512]{1,0:T(8,128)(2,1)S(1)}, u32[]{:S(2)}, u32[]{:S(2)}) %collective-permute-start.15) | collective-permute-done | bytes 524320 | tf_op jit(solution)/shard_map/ppermute | solution.py:75
  142.4 9.5 %collective-permute-done.16 = bf16[512,512]{1,0:T(8,128)(2,1)S(1)} collective-permute-done((bf16[512,512]{1,0:T(8,128)(2,1)S(1)}, bf16[512,512]{1,0:T(8,128)(2,1)S(1)}, u32[]{:S(2)}, u32[]{:S(2)}) %collective-permute-start.16) | collective-permute-done | bytes 524320 | tf_op jit(solution)/shard_map/ppermute | solution.py:102
  157.6 9.4 %collective-permute-done.17 = bf16[512,512]{1,0:T(8,128)(2,1)S(1)} collective-permute-done((bf16[512,512]{1,0:T(8,128)(2,1)S(1)}, bf16[512,512]{1,0:T(8,128)(2,1)S(1)}, u32[]{:S(2)}, u32[]{:S(2)}) %collective-permute-start.17) | collective-permute-done | bytes 524320 | tf_op jit(solution)/shard_map/ppermute | solution.py:102
  183.4 14.0 %collective-permute-done.21 = bf16[512,512]{1,0:T(8,128)(2,1)S(1)} collective-permute-done((bf16[512,512]{1,0:T(8,128)(2,1)}, bf16[512,512]{1,0:T(8,128)(2,1)S(1)}, u32[]{:S(2)}, u32[]{:S(2)}) %collective-permute-start.21) | collective-permute-done | bytes 524320 | tf_op jit(solution)/shard_map/ppermute | solution.py:105
  204.2 5.7 %collective-permute-done.22 = bf16[512,512]{1,0:T(8,128)(2,1)S(1)} collective-permute-done((bf16[512,512]{1,0:T(8,128)(2,1)S(1)}, bf16[512,512]{1,0:T(8,128)(2,1)S(1)}, u32[]{:S(2)}, u32[]{:S(2)}) %collective-permute-start.22) | collective-permute-done | bytes 524320 | tf_op jit(solution)/shard_map/ppermute | solution.py:74
  217.0 10.0 %collective-permute-done.26 = bf16[512,512]{1,0:T(8,128)(2,1)} collective-permute-done((bf16[512,512]{1,0:T(8,128)(2,1)S(1)}, bf16[512,512]{1,0:T(8,128)(2,1)}, u32[]{:S(2)}, u32[]{:S(2)}) %collective-permute-start.26) | collective-permute-done | bytes 524320 | tf_op jit(solution)/shard_map/ppermute | solution.py:75
  228.5 9.9 %collective-permute-done.27 = bf16[512,512]{1,0:T(8,128)(2,1)} collective-permute-done((bf16[512,512]{1,0:T(8,128)(2,1)}, bf16[512,512]{1,0:T(8,128)(2,1)}, u32[]{:S(2)}, u32[]{:S(2)}) %collective-permute-start.27) | collective-permute-done | bytes 524320 | tf_op jit(solution)/shard_map/ppermute | solution.py:75
  244.3 11.1 %fusion.94 = f32[512,2816]{1,0:T(8,128)} fusion(bf16[512,2048]{1,0:T(8,128)(2,1)S(1)} %fusion.24, bf16[2048,2816]{1,0:T(8,128)(2,1)} %all-gather.10.cloned.1.call-done), kind=kOutput, calls=%fused_computation.281 | convolution fusion | flops 5905580032 | bytes 19398656 | tf_op jit(solution)/shard_map/dot_general | solution.py:45
  255.3 9.5 %multiply_convert_fusion.1 = (bf16[512,1408]{1,0:T(8,128)(2,1)S(1)}, bf16[512,1408]{1,0:T(8,128)(2,1)S(1)}, bf16[512,1408]{1,0:T(8,128)(2,1)S(1)}) fusion(f32[512,2816]{1,0:T(8,128)} %fusion.94, bf16[1408,2048]{1,0:T(8,128)(2,1)} %all-gather.12.cloned.1.call-done, bf16[512,512]{1,0:T(8,128)(2,1)} %copy-done.33, bf16[512,512]{1,0:T(8,128)(2,1)} %copy-done.31, ...), kind=kOutput, calls=%fused_computation.52 | convolution fusion | flops 2972712960 | bytes 17956864 | tf_op jit(solution)/shard_map/dot_general | solution.py:45
  294.1 18.6 %reduce-scatter.4.cloned.1.call-done = bf16[512,512]{1,0:T(8,128)(2,1)} async-done(((bf16[512,2048]{1,0:T(8,128)(2,1)}), bf16[512,512]{1,0:T(8,128)(2,1)}) %reduce-scatter.4.cloned.1.call-update) | async-done | bytes 524304 | tf_op jit(solution)/shard_map/reduce_scatter | solution.py:116
  326.8 7.4 %convolution_convert_fusion.3 = bf16[512,2048]{1,0:T(8,128)(2,1)} fusion(bf16[512,1408]{1,0:T(8,128)(2,1)S(1)} %get-tuple-element.168, bf16[1408,2048]{1,0:T(8,128)(2,1)} %all-gather.12.cloned.1.call-done), kind=kOutput, calls=%fused_computation.50 | convolution fusion | flops 2953838592 | bytes 9306112 | tf_op jit(solution)/shard_map/dot_general | solution.py:45
  335.7 5.7 add_convert_fusion.1
  341.4 17.6 %all-gather.14.cloned.1.call-done = bf16[512,2048]{1,0:T(8,128)(2,1)} async-done(((bf16[512,512]{1,0:T(8,128)(2,1)}), bf16[512,2048]{1,0:T(8,128)(2,1)}) %all-gather.14.cloned.1.call-update) | async-done | bytes 2097168 | tf_op jit(solution)/shard_map/all_gather | solution.py:112
  370.9 9.9 %fusion.33 = f32[2,1280,64]{1,2,0:T(8,128)} fusion(bf16[2,256,8,64]{1,3,2,0:T(8,128)(2,1)S(1)} %copy.86, f32[2,1280,256,8]{2,1,3,0:T(8,128)} %copy-done, f32[2,8,256]{2,1,0:T(8,128)S(1)} %copy-done.90, pred[2,256,1280]{1,2,0:T(8,128)(4,1)S(1)} %copy-done.22), kind=kOutput, calls=%fused_computation.58 | convolution fusion | flops 692060160 | bytes 22822912 | tf_op jit(solution)/shard_map/bhlm,blhd->bmd/dot_general | solution.py:184
  380.7 11.1 %fusion.2 = bf16[2,8,256,1280]{2,3,1,0:T(8,128)(2,1)S(1)} fusion(f32[2,1280,256,8]{2,1,3,0:T(8,128)} %copy-done, bf16[2,256,8,64]{1,3,2,0:T(8,128)(2,1)} %copy-done.46, f32[2,8,256]{2,1,0:T(8,128)S(1)} %bitcast.221, f32[2,8,256]{2,1,0:T(8,128)S(1)} %copy-done.90, pred[2,256,1280]{1,2,0:T(8,128)(4,1)} %copy-done.21, bf16[2,1280,128]{1,2,0:T(8,128)(2,1)} %copy-done.65), kind=kOutput, calls=%fused_computation.3 | convolution fusion | flops 707788800 | bytes 32997376 | tf_op jit(solution)/shard_map/blhd,bmd->bhlm/dot_general | solution.py:185
  447.1 8.8 %reduce-scatter.6.cloned.1.call-done = bf16[512,512]{1,0:T(8,128)(2,1)} async-done(((bf16[512,2048]{1,0:T(8,128)(2,1)}), bf16[512,512]{1,0:T(8,128)(2,1)}) %reduce-scatter.6.cloned.1.call-update) | async-done | bytes 524304 | tf_op jit(solution)/shard_map/reduce_scatter | solution.py:116
  468.8 8.2 %collective-permute-done.47 = bf16[256,1408]{1,0:T(8,128)(2,1)S(1)} collective-permute-done((bf16[256,1408]{1,0:T(8,128)(2,1)S(1)}, bf16[256,1408]{1,0:T(8,128)(2,1)S(1)}, u32[]{:S(2)}, u32[]{:S(2)}) %collective-permute-start.47) | collective-permute-done | bytes 720928 | tf_op jit(solution)/shard_map/ppermute | solution.py:57
  482.4 13.8 %collective-permute-done.48 = bf16[256,1408]{1,0:T(8,128)(2,1)S(1)} collective-permute-done((bf16[256,1408]{1,0:T(8,128)(2,1)S(1)}, bf16[256,1408]{1,0:T(8,128)(2,1)S(1)}, u32[]{:S(2)}, u32[]{:S(2)}) %collective-permute-start.48) | collective-permute-done | bytes 720928 | tf_op jit(solution)/shard_map/ppermute | solution.py:57
  499.7 8.2 %collective-permute-done.51 = bf16[1408,256]{1,0:T(8,128)(2,1)S(1)} collective-permute-done((bf16[1408,256]{1,0:T(8,128)(2,1)S(1)}, bf16[1408,256]{1,0:T(8,128)(2,1)S(1)}, u32[]{:S(2)}, u32[]{:S(2)}) %collective-permute-start.51) | collective-permute-done | bytes 720928 | tf_op jit(solution)/shard_map/ppermute | solution.py:57
  510.3 16.9 %collective-permute-done.52 = bf16[1408,256]{1,0:T(8,128)(2,1)S(1)} collective-permute-done((bf16[1408,256]{1,0:T(8,128)(2,1)S(1)}, bf16[1408,256]{1,0:T(8,128)(2,1)S(1)}, u32[]{:S(2)}, u32[]{:S(2)}) %collective-permute-start.52) | collective-permute-done | bytes 720928 | tf_op jit(solution)/shard_map/ppermute | solution.py:57
  543.1 10.2 %collective-permute-done.38 = bf16[256,768]{1,0:T(8,128)(2,1)S(1)} collective-permute-done((bf16[256,768]{1,0:T(8,128)(2,1)S(1)}, bf16[256,768]{1,0:T(8,128)(2,1)S(1)}, u32[]{:S(2)}, u32[]{:S(2)}) %collective-permute-start.38) | collective-permute-done | bytes 393248 | tf_op jit(solution)/shard_map/ppermute | solution.py:57
  (459 shorter events, 292.5 us)
Async XLA Ops:
  7.2 66.6 %all-gather.6.cloned.1.call-start = ((), (), s32[]{:S(2)}) async-start(), calls=%async_computation.3 | async-start | bytes 3538944 | tf_op jit(solution)/shard_map/all_gather | solution.py:226
  12.3 122.8 %all-gather.8.cloned.1.call-start = ((), (), s32[]{:S(2)}) async-start(), calls=%async_computation.4 | async-start | bytes 2359296 | tf_op jit(solution)/shard_map/all_gather | solution.py:233
  63.6 180.7 %all-gather.10.cloned.1.call-start = ((), (), s32[]{:S(2)}) async-start(), calls=%async_computation.5 | async-start | bytes 12976128 | tf_op jit(solution)/shard_map/all_gather | solution.py:235
  66.6 188.7 %all-gather.12.cloned.1.call-start = ((), (), s32[]{:S(2)}) async-start(), calls=%async_computation.6 | async-start | bytes 6488064 | tf_op jit(solution)/shard_map/all_gather | solution.py:238
  69.7 27.1 %collective-permute-start.10 = (bf16[512,512]{1,0:T(8,128)(2,1)}, bf16[512,512]{1,0:T(8,128)(2,1)}, u32[]{:S(2)}, u32[]{:S(2)}) collective-permute-start(bf16[512,512]{1,0:T(8,128)(2,1)} %bitcast.213), channel_id=1, source_target_pairs={{0,1},{1,2},{2,3},{4,5},{5,6},{6,7},{8,9},{9,10},{10,11},{12,13},{... | collective-permute-start | bytes 1572872 | tf_op jit(solution)/shard_map/ppermute | solution.py:74
  71.8 26.3 %collective-permute-start.13 = (bf16[512,512]{1,0:T(8,128)(2,1)}, bf16[512,512]{1,0:T(8,128)(2,1)}, u32[]{:S(2)}, u32[]{:S(2)}) collective-permute-start(bf16[512,512]{1,0:T(8,128)(2,1)} %bitcast.214), channel_id=1, source_target_pairs={{1,0},{2,1},{3,2},{5,4},{6,5},{7,6},{9,8},{10,9},{11,10},{13,12},{... | collective-permute-start | bytes 1572872 | tf_op jit(solution)/shard_map/ppermute | solution.py:75
  73.7 239.0 %reduce-scatter.4.cloned.1.call-start = ((), (), s32[]{:S(2)}) async-start(), calls=%async_computation.7 | async-start | bytes 2621440 | tf_op jit(solution)/shard_map/reduce_scatter | solution.py:116
  273.1 86.0 %all-gather.14.cloned.1.call-start = ((), (), s32[]{:S(2)}) async-start(), calls=%async_computation.8 | async-start | bytes 2621440 | tf_op jit(solution)/shard_map/all_gather | solution.py:112
  284.5 51.3 %collective-permute-start.50 = (bf16[1408,1024]{1,0:T(8,128)(2,1)}, bf16[1408,1024]{1,0:T(8,128)(2,1)}, u32[]{:S(2)}, u32[]{:S(2)}) collective-permute-start(bf16[1408,1024]{1,0:T(8,128)(2,1)} %convolution_convert_fusion), channel_id=1, source_target_pairs={{0,4},{4,0},{8,12},{12,8},{16,20},{20,16},{24,28},{28,24},{1,5},{5... | collective-permute-start | bytes 8650760 | tf_op jit(solution)/shard_map/ppermute | solution.py:57
  312.7 143.1 %reduce-scatter.6.cloned.1.call-start = ((), (), s32[]{:S(2)}) async-start(), calls=%async_computation.9 | async-start | bytes 2621440 | tf_op jit(solution)/shard_map/reduce_scatter | solution.py:116
  334.2 127.4 %collective-permute-start.44 = (bf16[256,1408]{1,0:T(8,128)(2,1)}, bf16[256,1408]{1,0:T(8,128)(2,1)}, u32[]{:S(2)}, u32[]{:S(2)}) collective-permute-start(bf16[256,1408]{1,0:T(8,128)(2,1)} %get-tuple-element.185), channel_id=1, source_target_pairs={{0,8},{4,12},{8,0},{12,4},{16,24},{20,28},{24,16},{28,20},{1,9},{5... | collective-permute-start | bytes 2162696 | tf_op jit(solution)/shard_map/ppermute | solution.py:57
  407.0 149.9 %reduce-scatter.8.cloned.1.call-start = ((), (), s32[]{:S(2)}) async-start(), calls=%async_computation.10 | async-start | bytes 2621440 | tf_op jit(solution)/shard_map/reduce_scatter | solution.py:116
  412.6 53.1 %collective-permute-start.45 = (bf16[256,1408]{1,0:T(8,128)(2,1)}, bf16[256,1408]{1,0:T(8,128)(2,1)}, u32[]{:S(2)}, u32[]{:S(2)}) collective-permute-start(bf16[256,1408]{1,0:T(8,128)(2,1)} %get-tuple-element.184), channel_id=1, source_target_pairs={{0,16},{4,20},{8,24},{12,28},{16,0},{20,4},{24,8},{28,12},{1,17},{... | collective-permute-start | bytes 2162696 | tf_op jit(solution)/shard_map/ppermute | solution.py:57
  417.7 49.5 %collective-permute-start.46 = (bf16[256,1408]{1,0:T(8,128)(2,1)}, bf16[256,1408]{1,0:T(8,128)(2,1)}, u32[]{:S(2)}, u32[]{:S(2)}) collective-permute-start(bf16[256,1408]{1,0:T(8,128)(2,1)} %get-tuple-element.183), channel_id=1, source_target_pairs={{0,24},{4,28},{8,16},{12,20},{16,8},{20,12},{24,0},{28,4},{1,25},{... | collective-permute-start | bytes 2162696 | tf_op jit(solution)/shard_map/ppermute | solution.py:57
  419.9 37.9 %collective-permute-start.40 = (bf16[512,1024]{1,0:T(8,128)(2,1)}, bf16[512,1024]{1,0:T(8,128)(2,1)}, u32[]{:S(2)}, u32[]{:S(2)}) collective-permute-start(bf16[512,1024]{1,0:T(8,128)(2,1)} %convolution_convert_fusion.5), channel_id=1, source_target_pairs={{0,4},{4,0},{8,12},{12,8},{16,20},{20,16},{24,28},{28,24},{1,5},{5... | collective-permute-start | bytes 3145736 | tf_op jit(solution)/shard_map/ppermute | solution.py:57
  461.6 34.5 %collective-permute-start.48 = (bf16[256,1408]{1,0:T(8,128)(2,1)S(1)}, bf16[256,1408]{1,0:T(8,128)(2,1)S(1)}, u32[]{:S(2)}, u32[]{:S(2)}) collective-permute-start(bf16[256,1408]{1,0:T(8,128)(2,1)S(1)} %copy-done.69), channel_id=1, source_target_pairs={{0,16},{4,20},{8,24},{12,28},{16,0},{20,4},{24,8},{28,12},{1,17},{... | collective-permute-start | bytes 2162696 | tf_op jit(solution)/shard_map/ppermute | solution.py:57
  463.2 33.5 %collective-permute-start.49 = (bf16[256,1408]{1,0:T(8,128)(2,1)S(1)}, bf16[256,1408]{1,0:T(8,128)(2,1)S(1)}, u32[]{:S(2)}, u32[]{:S(2)}) collective-permute-start(bf16[256,1408]{1,0:T(8,128)(2,1)S(1)} %copy-done.68), channel_id=1, source_target_pairs={{0,24},{4,28},{8,16},{12,20},{16,8},{20,12},{24,0},{28,4},{1,25},{... | collective-permute-start | bytes 2162696 | tf_op jit(solution)/shard_map/ppermute | solution.py:57
  465.7 42.2 %collective-permute-start.51 = (bf16[1408,256]{1,0:T(8,128)(2,1)S(1)}, bf16[1408,256]{1,0:T(8,128)(2,1)S(1)}, u32[]{:S(2)}, u32[]{:S(2)}) collective-permute-start(bf16[1408,256]{1,0:T(8,128)(2,1)S(1)} %copy-done.73), channel_id=1, source_target_pairs={{0,8},{4,12},{8,0},{12,4},{16,24},{20,28},{24,16},{28,20},{1,9},{5... | collective-permute-start | bytes 2162696 | tf_op jit(solution)/shard_map/ppermute | solution.py:57
  467.3 59.9 %collective-permute-start.52 = (bf16[1408,256]{1,0:T(8,128)(2,1)S(1)}, bf16[1408,256]{1,0:T(8,128)(2,1)S(1)}, u32[]{:S(2)}, u32[]{:S(2)}) collective-permute-start(bf16[1408,256]{1,0:T(8,128)(2,1)S(1)} %copy-done.72), channel_id=1, source_target_pairs={{0,16},{4,20},{8,24},{12,28},{16,0},{20,4},{24,8},{28,12},{1,17},{... | collective-permute-start | bytes 2162696 | tf_op jit(solution)/shard_map/ppermute | solution.py:57
  477.0 50.6 %collective-permute-start.53 = (bf16[1408,256]{1,0:T(8,128)(2,1)S(1)}, bf16[1408,256]{1,0:T(8,128)(2,1)S(1)}, u32[]{:S(2)}, u32[]{:S(2)}) collective-permute-start(bf16[1408,256]{1,0:T(8,128)(2,1)S(1)} %copy-done.71), channel_id=1, source_target_pairs={{0,24},{4,28},{8,16},{12,20},{16,8},{20,12},{24,0},{28,4},{1,25},{... | collective-permute-start | bytes 2162696 | tf_op jit(solution)/shard_map/ppermute | solution.py:57
  496.2 33.5 %collective-permute-start.41 = (bf16[512,256]{1,0:T(8,128)(2,1)S(1)}, bf16[512,256]{1,0:T(8,128)(2,1)S(1)}, u32[]{:S(2)}, u32[]{:S(2)}) collective-permute-start(bf16[512,256]{1,0:T(8,128)(2,1)S(1)} %get-tuple-element.236), channel_id=1, source_target_pairs={{0,8},{4,12},{8,0},{12,4},{16,24},{20,28},{24,16},{28,20},{1,9},{5... | collective-permute-start | bytes 786440 | tf_op jit(solution)/shard_map/ppermute | solution.py:57
  496.7 41.6 %collective-permute-start.42 = (bf16[512,256]{1,0:T(8,128)(2,1)S(1)}, bf16[512,256]{1,0:T(8,128)(2,1)S(1)}, u32[]{:S(2)}, u32[]{:S(2)}) collective-permute-start(bf16[512,256]{1,0:T(8,128)(2,1)S(1)} %get-tuple-element.235), channel_id=1, source_target_pairs={{0,16},{4,20},{8,24},{12,28},{16,0},{20,4},{24,8},{28,12},{1,17},{... | collective-permute-start | bytes 786440 | tf_op jit(solution)/shard_map/ppermute | solution.py:57
  507.9 30.4 %collective-permute-start.43 = (bf16[512,256]{1,0:T(8,128)(2,1)S(1)}, bf16[512,256]{1,0:T(8,128)(2,1)S(1)}, u32[]{:S(2)}, u32[]{:S(2)}) collective-permute-start(bf16[512,256]{1,0:T(8,128)(2,1)S(1)} %get-tuple-element.234), channel_id=1, source_target_pairs={{0,24},{4,28},{8,16},{12,20},{16,8},{20,12},{24,0},{28,4},{1,25},{... | collective-permute-start | bytes 786440 | tf_op jit(solution)/shard_map/ppermute | solution.py:57
  527.6 25.7 %collective-permute-start.38 = (bf16[256,768]{1,0:T(8,128)(2,1)S(1)}, bf16[256,768]{1,0:T(8,128)(2,1)S(1)}, u32[]{:S(2)}, u32[]{:S(2)}) collective-permute-start(bf16[256,768]{1,0:T(8,128)(2,1)S(1)} %get-tuple-element.219), channel_id=1, source_target_pairs={{0,16},{4,20},{8,24},{12,28},{16,0},{20,4},{24,8},{28,12},{1,17},{... | collective-permute-start | bytes 1179656 | tf_op jit(solution)/shard_map/ppermute | solution.py:57
  (135 other events, 1271.2 us)
Sparse Core Ops, SparseCore 0:
  12.4 34.8 all-gather.5
  63.7 26.1 all-gather.7
  92.4 69.1 all-gather.9
  163.3 44.2 all-gather.11
  273.2 39.4 reduce-scatter.3
  314.1 44.8 all-gather.13
  407.1 48.7 reduce-scatter.5
  458.2 42.8 reduce-scatter.7
where the time goes:
time: 578 us; the launch traced here: 568 us
  waiting for transfers between devices  234 us (40%)
  matrix products  122 us (21%)
  starting transfers between devices  88.7 us (15%)
  other arithmetic  65 us (11%)
  local copies, waits for them, and re-layouts  41.1 us (7%)
  between operations  16.6 us (3%)
    ppermute x22, waiting for transfers between devices, exchange(): lax.ppermute(block, axis, [(i, i ^ mask) for i in range(lax.axis_size(axi...  73.8 us
    ppermute x9, waiting for transfers between devices, tp_gather(): lax.ppermute(upper, 'tp', [(i, i - 1) for i in range(1, size - step + 1)])  61.6 us
    dot_general x25, matrix products, dot_tn(): lax.dot_general(left, right, (((0,), (0,)), ((), ())), preferred_element_...  38.1 us
    dot_general x5, matrix products, dot_nn(): return jnp.dot(left, right, preferred_element_type=F32)  32.6 us
    ppermute x22, starting transfers between devices, exchange(): lax.ppermute(block, axis, [(i, i ^ mask) for i in range(lax.axis_size(axi...  29 us
    reduce_scatter x3, waiting for transfers between devices, queue_scatter_sum(): lax.psum_scatter(partial.astype(BF16), 'tp', scatter_dimension=1, tiled=T...  27.4 us
    ppermute x3, waiting for transfers between devices, tp_scatter_sum(): lax.ppermute(to_upper.astype(BF16), 'tp', [(i, i + 1) for i in range(min(...  23.9 us
    all_gather x1, waiting for transfers between devices, queue_gather(): return lax.all_gather(part, 'tp', axis=1, tiled=True)  17.6 us
  transfers between devices with their start and end apart: 62, of which 26 were waited for; matrix products, arithmetic and copies ran while one was open for 34% of the time, Pallas kernels for 0%

commit v1 on v0

--- a/solution.py
+++ b/solution.py
@@ -69,8 +69,8 @@
     up, down = [part], [part]
     for step in range(1, size):
         lower, upper = up[-1], down[-1]
-        if earlier and step == 2:
-            lower, upper = after(lower, *earlier), after(upper, *earlier)
+        if 2 <= step < len(earlier) + 2:
+            lower, upper = lax.optimization_barrier((lower, upper, earlier[step - 2]))[:2]
         up.append(lax.ppermute(lower, "tp", [(i, i + 1) for i in range(step - 1, size - 1)]))
         down.append(lax.ppermute(upper, "tp", [(i, i - 1) for i in range(1, size - step + 1)]))
     slots = []
@@ -84,28 +84,44 @@
     return jnp.concatenate(slots, 1)
 
 
+def tp_gather_far(part, *earlier):
+    size = lax.axis_size("tp")
+    index = lax.axis_index("tp")
+    held = [part]
+    bit = size // 2
+    while bit:
+        send = held[0][None] if len(held) == 1 else jnp.stack(held)
+        other = exchange(send, "tp", bit)
+        if earlier and bit > 1:
+            other = after(other, *earlier)
+        low = (index & bit) == 0
+        merged = []
+        for slot, block in enumerate(held):
+            merged.append(jnp.where(low, block, other[slot]))
+            merged.append(jnp.where(low, other[slot], block))
+        held = merged
+        bit //= 2
+    return jnp.concatenate(held, 1)
+
+
 def tp_scatter_sum(partial):
     size = lax.axis_size("tp")
     index = lax.axis_index("tp")
     width = partial.shape[1] // size
-
-    def slot(at):
-        at = jnp.clip(at, 0, size - 1)
-        return lax.dynamic_slice_in_dim(partial, at * width, width, 1)
-
-    total = slot(index)
-    lower = upper = None
-    for step in range(1, size):
-        to_upper, to_lower = slot(index + size - step), slot(index - size + step)
-        if lower is not None:
-            to_upper, to_lower = to_upper + lower.astype(F32), to_lower + upper.astype(F32)
-        lower = lax.ppermute(
-            to_upper.astype(BF16), "tp", [(i, i + 1) for i in range(min(step, size - 1))]
+    held = [partial[:, s * width : (s + 1) * width] for s in range(size)]
+    bit = 1
+    while bit < size:
+        low = (index & bit) == 0
+        send = jnp.stack(
+            [jnp.where(low, b, a).astype(BF16) for a, b in zip(held[0::2], held[1::2])]
         )
-        upper = lax.ppermute(
-            to_lower.astype(BF16), "tp", [(i, i - 1) for i in range(size - step, size)]
-        )
-    return total + lower.astype(F32) + upper.astype(F32)
+        other = exchange(send, "tp", bit)
+        held = [
+            jnp.where(low, a, b) + other[slot].astype(F32)
+            for slot, (a, b) in enumerate(zip(held[0::2], held[1::2]))
+        ]
+        bit *= 2
+    return held[0]
 
 
 def queue_gather(part):
@@ -216,6 +232,7 @@
     score_scale = HEAD_SIZE ** (-0.5)
     back = min(group_size - 1, -(-(DOC_MAX - 1) // row_count))
     column_start = lax.axis_index("tp") * local_width
+    shard_rows = w_query.shape[0]
 
     gains = jnp.stack([attn_norm, mlp_norm], 1)
     gains = jnp.pad(gains, ((0, 0), (0, GAIN_COLUMNS - 2)))
@@ -229,9 +246,17 @@
     gain_one, gain_two = gain_rows[0], gain_rows[1]
     rows = batch_count * row_count
     tokens_own = tokens.reshape(rows, local_width)
-    tokens_full = tp_gather(tokens_own)
+    gate_up_shard = lax.optimization_barrier(jnp.concatenate([w_gate, w_up], 1))
+    tables, allowed, gain_one, gain_two = lax.optimization_barrier(
+        (
+            rope_tables(positions.reshape(rows), HEAD_SIZE),
+            allowed_keys(positions, row_count, back),
+            gain_one,
+            gain_two,
+        )
+    )
+    tokens_full = tp_gather(tokens_own, gate_up_shard, gain_one)
     out_weight = lax.all_gather(after(w_out, tokens_full), "fsdp", axis=1, tiled=True)
-    gate_up_shard = lax.optimization_barrier(jnp.concatenate([w_gate, w_up], 1))
     gate_up_weight = lax.all_gather(
         after(gate_up_shard, tokens_full), "fsdp", axis=0, tiled=True
     )
@@ -243,8 +268,6 @@
     scale_one = lax.rsqrt(jnp.mean(inputs * inputs, -1, keepdims=True) + NORM_EPSILON)
     normed_one = (inputs * scale_one * gain_one).astype(BF16)
     projected = dot_nn(normed_one, project_weight)
-    tables = rope_tables(positions.reshape(rows), HEAD_SIZE)
-    allowed = allowed_keys(positions, row_count, back)
     query_rotated = by_batch(
         apply_rotary(
             projected[:, :query_width].reshape(rows, head_count, HEAD_SIZE), *tables
@@ -256,7 +279,7 @@
     pairs = by_batch(
         jnp.concatenate([key_rotated, projected[:, query_width + HEAD_SIZE :].astype(BF16)], -1)
     )
-    grad_in = tp_gather(after(out_grad.reshape(rows, local_width), tokens_full), pairs)
+    grad_in = tp_gather_far(after(out_grad.reshape(rows, local_width), tokens_full), pairs)
     window = [passed_along(pairs, "fsdp", o * stride) for o in range(back, 0, -1)]
     window = jnp.concatenate(window + [pairs], 1)
     keys, values = window[..., :HEAD_SIZE], window[..., HEAD_SIZE:]
@@ -290,7 +313,8 @@
     grads_order = owner_order(grad_in)
     down_terms, _ = owner_terms(grads_order, lambda block: dot_tn(activated, block), 1)
     grad_normed_two = queue_gather(after(partial_two, *gate_sent, *up_sent))
-    mlp_own = queue_scatter_sum(after(dot_nn(activated, down_weight).astype(BF16), grad_normed_two))
+    mlp_partial = dot_nn(activated, down_weight).astype(BF16)
+    mlp_own = queue_scatter_sum(after(mlp_partial, grad_normed_two))
     output = (middle_own + mlp_own.astype(F32)).astype(BF16)
 
     gain_one_own = lax.dynamic_slice_in_dim(gain_one, column_start, local_width, 0)
@@ -332,43 +356,39 @@
     small = jnp.concatenate([norm_sum_one, jnp.sum(weighted * gain_one, -1) / full_width])
     for bit in range((lax.axis_size("tp") - 1).bit_length()):
         small = small + exchange(small, "tp", 1 << bit)
-    norm_sum_one, row_mean = small[:full_width], small[full_width:, None]
+    row_mean = small[full_width:, None]
+    norm_sums = jnp.concatenate([small[:full_width], norm_sum_two])
+    for bit in range((lax.axis_size("fsdp") - 1).bit_length()):
+        norm_sums = norm_sums + exchange(norm_sums, "fsdp", 1 << bit)
     grad_middle_own = lax.dynamic_slice_in_dim(grad_middle, column_start, local_width, 1)
     input_grad = (
         grad_middle_own
         + scale_one * (summed.astype(F32) * gain_one_own)
         - tokens_own.astype(F32) * (scale_one * scale_one * scale_one) * row_mean
     )
-    middle_order = owner_order(middle_low)
-    out_terms, _ = owner_terms(middle_order, lambda block: dot_tn(heads_out, block), 1)
-    norm_order = owner_order(jnp.stack([norm_sum_one, norm_sum_two]))
     normed_one_order = owner_order(normed_one)
     project_terms, project_sent = owner_terms(
-        list(zip(normed_one_order, norm_order)),
-        lambda pair: jnp.concatenate(
-            [
-                dot_tn(pair[0], grad_projected),
-                jnp.pad(pair[1].T, ((0, 0), (0, GAIN_COLUMNS - 2))),
-            ],
-            1,
-        ),
-        0,
-    )
+        normed_one_order, lambda block: dot_tn(block, grad_projected), 0
+    )
+    middle_order = owner_order(after(middle_low, *project_sent))
+    out_terms, out_sent = owner_terms(middle_order, lambda block: dot_tn(heads_out, block), 1)
     grad_scale = (batch_count * row_count * lax.axis_size("fsdp")) ** (-0.5)
-    down_sum = owner_total(down_terms, *project_sent)
-    gate_sum = owner_total(gate_terms, *project_sent)
-    up_sum = owner_total(up_terms, *project_sent)
-    out_sum = owner_total(out_terms, *project_sent)
+    norm_start = lax.axis_index("fsdp") * shard_rows
+    norm_sums = norm_sums * grad_scale
+    down_sum = owner_total(down_terms, *out_sent)
+    gate_sum = owner_total(gate_terms, *out_sent)
+    up_sum = owner_total(up_terms, *out_sent)
+    out_sum = owner_total(out_terms, *out_sent)
     project_sum = owner_total(project_terms) * grad_scale
     return (
         by_batch(output),
         by_batch(input_grad),
-        project_sum[:, project_width],
+        lax.dynamic_slice_in_dim(norm_sums, norm_start, shard_rows, 0),
         project_sum[:, :query_width],
         project_sum[:, query_width : query_width + HEAD_SIZE],
-        project_sum[:, query_width + HEAD_SIZE : project_width],
+        project_sum[:, query_width + HEAD_SIZE :],
         out_sum * grad_scale,
-        project_sum[:, project_width + 1],
+        lax.dynamic_slice_in_dim(norm_sums, full_width + norm_start, shard_rows, 0),
         gate_sum * grad_scale,
         up_sum * grad_scale,
         down_sum * grad_scale,

time: 578 us -> 598 us (1.035)
  waiting for transfers between devices: 234 us -> 294 us
  starting transfers between devices: 88.7 us -> 60.1 us
    ppermute x22 -> x29, waiting for transfers between devices: 73.8 us -> 177 us  [exchange(): lax.ppermute(block, axis, [(i, i ^ mask) for i in range(lax.axis_size(axi...]
    ppermute x6 -> x0, waiting for transfers between devices: 38 us -> none  [the longest x3 23.9 us: tp_scatter_sum(): lax.ppermute(to_upper.astype(BF16), 'tp', [(i, i + 1) for i in range(min(...]
    ppermute x9 -> x6, waiting for transfers between devices: 61.6 us -> 46.9 us  [tp_gather(): lax.ppermute(upper, 'tp', [(i, i - 1) for i in range(1, size - step + 1)])]
    ppermute x6 -> x0, starting transfers between devices: 13.8 us -> none  [the longest x3 11 us: tp_scatter_sum(): lax.ppermute(to_upper.astype(BF16), 'tp', [(i, i + 1) for i in range(min(...]
    all_gather x1, waiting for transfers between devices: 0.02 us -> 11.7 us  [shards(): first_full = lax.all_gather(first_shard, 'fsdp', axis=0, tiled=True)]
    reduce_scatter x3, waiting for transfers between devices: 27.4 us -> 19.5 us  [queue_scatter_sum(): lax.psum_scatter(partial.astype(BF16), 'tp', scatter_dimension=1, tiled=T...]
    convert_element_type x4 -> x2, other arithmetic: 7.39 us -> 1.1 us  [the longest x1 0.95 us: shards(): output = (middle_own + mlp_own.astype(F32)).astype(BF16)]
    ppermute x9 -> x6, starting transfers between devices: 16.4 us -> 10.6 us  [tp_gather(): lax.ppermute(lower, 'tp', [(i, i + 1) for i in range(step - 1, size - 1)])]
  transfers between devices with their start and end apart: 62 -> 57, of which waited for: 26 -> 26; matrix products, arithmetic and copies ran while one was open for 34% -> 31% of each run, Pallas kernels for 0% -> 0%
where the time goes in v1:
time: 598 us; the launch traced here: 590 us
  waiting for transfers between devices  294 us (49%)
  matrix products  123 us (21%)
  starting transfers between devices  60.1 us (10%)
  other arithmetic  59.3 us (10%)
  local copies, waits for them, and re-layouts  36.7 us (6%)
  between operations  16.2 us (3%)
    ppermute x29, waiting for transfers between devices, exchange(): lax.ppermute(block, axis, [(i, i ^ mask) for i in range(lax.axis_size(axi...  177 us
    ppermute x6, waiting for transfers between devices, tp_gather(): lax.ppermute(upper, 'tp', [(i, i - 1) for i in range(1, size - step + 1)])  46.9 us
    dot_general x25, matrix products, dot_tn(): lax.dot_general(left, right, (((0,), (0,)), ((), ())), preferred_element_...  37.7 us
    dot_general x5, matrix products, dot_nn(): return jnp.dot(left, right, preferred_element_type=F32)  32.6 us
    ppermute x29, starting transfers between devices, exchange(): lax.ppermute(block, axis, [(i, i ^ mask) for i in range(lax.axis_size(axi...  24.1 us
    all_gather x1, waiting for transfers between devices, queue_gather(): return lax.all_gather(part, 'tp', axis=1, tiled=True)  20.1 us
    reduce_scatter x3, waiting for transfers between devices, queue_scatter_sum(): lax.psum_scatter(partial.astype(BF16), 'tp', scatter_dimension=1, tiled=T...  19.5 us
    ppermute x8, starting transfers between devices, passed_along(): return lax.ppermute(block, axis, route)  16.4 us
  transfers between devices with their start and end apart: 57, of which 26 were waited for; matrix products, arithmetic and copies ran while one was open for 31% of the time, Pallas kernels for 0%

profile of v1, /device:TPU:0, one launch (start us, length us, event | category | flops | bytes accessed | tf_op | source)
XLA Modules:
  0.0 589.6 jit_solution(10220029776555563115)
XLA Ops:
  12.5 5.8 collective-permute-start
  35.8 11.7 %all-gather.6.cloned.1.call-done = bf16[2048,768]{1,0:T(8,128)(2,1)} async-done(((bf16[256,768]{1,0:T(8,128)(2,1)}), bf16[2048,768]{1,0:T(8,128)(2,1)}) %all-gather.6.cloned.1.call-update) | async-done | bytes 3145744 | tf_op jit(solution)/shard_map/all_gather | solution.py:243
  52.7 13.6 %collective-permute-done.5 = bf16[512,512]{1,0:T(8,128)(2,1)} collective-permute-done((bf16[512,512]{1,0:T(8,128)(2,1)S(1)}, bf16[512,512]{1,0:T(8,128)(2,1)}, u32[]{:S(2)}, u32[]{:S(2)}) %collective-permute-start.5) | collective-permute-done | bytes 524320 | tf_op jit(solution)/shard_map/ppermute | solution.py:75
  107.9 10.0 %collective-permute-done.10 = bf16[1,512,512]{2,1,0:T(8,128)(2,1)} collective-permute-done((bf16[1,512,512]{2,1,0:T(8,128)(2,1)S(1)}, bf16[1,512,512]{2,1,0:T(8,128)(2,1)}, u32[]{:S(2)}, u32[]{:S(2)}) %collective-permute-start.10) | collective-permute-done | bytes 524320 | tf_op jit(solution)/shard_map/ppermute | solution.py:57
  119.2 5.4 fusion.41
  125.4 18.9 %collective-permute-done.11 = bf16[2,512,512]{2,1,0:T(8,128)(2,1)} collective-permute-done((bf16[2,512,512]{2,1,0:T(8,128)(2,1)S(1)}, bf16[2,512,512]{2,1,0:T(8,128)(2,1)}, u32[]{:S(2)}, u32[]{:S(2)}) %collective-permute-start.11) | collective-permute-done | bytes 1048608 | tf_op jit(solution)/shard_map/ppermute | solution.py:57
  151.4 23.8 %collective-permute-done.12 = bf16[2,512,512]{2,1,0:T(8,128)(2,1)S(1)} collective-permute-done((bf16[2,512,512]{2,1,0:T(8,128)(2,1)S(1)}, bf16[2,512,512]{2,1,0:T(8,128)(2,1)S(1)}, u32[]{:S(2)}, u32[]{:S(2)}) %collective-permute-start.12) | collective-permute-done | bytes 1048608 | tf_op jit(solution)/shard_map/ppermute | solution.py:57
  176.6 23.5 %collective-permute-done.13 = bf16[1,512,512]{2,1,0:T(8,128)(2,1)S(1)} collective-permute-done((bf16[1,512,512]{2,1,0:T(8,128)(2,1)S(1)}, bf16[1,512,512]{2,1,0:T(8,128)(2,1)S(1)}, u32[]{:S(2)}, u32[]{:S(2)}) %collective-permute-start.13) | collective-permute-done | bytes 524320 | tf_op jit(solution)/shard_map/ppermute | solution.py:57
  204.5 9.8 %collective-permute-done.14 = bf16[512,512]{1,0:T(8,128)(2,1)S(1)} collective-permute-done((bf16[512,512]{1,0:T(8,128)(2,1)S(1)}, bf16[512,512]{1,0:T(8,128)(2,1)S(1)}, u32[]{:S(2)}, u32[]{:S(2)}) %collective-permute-start.14) | collective-permute-done | bytes 524320 | tf_op jit(solution)/shard_map/ppermute | solution.py:74
  221.2 11.6 %collective-permute-done.18 = bf16[512,512]{1,0:T(8,128)(2,1)S(1)} collective-permute-done((bf16[512,512]{1,0:T(8,128)(2,1)S(1)}, bf16[512,512]{1,0:T(8,128)(2,1)S(1)}, u32[]{:S(2)}, u32[]{:S(2)}) %collective-permute-start.18) | collective-permute-done | bytes 524320 | tf_op jit(solution)/shard_map/ppermute | solution.py:75
  234.4 12.1 %collective-permute-done.19 = bf16[512,512]{1,0:T(8,128)(2,1)} collective-permute-done((bf16[512,512]{1,0:T(8,128)(2,1)S(1)}, bf16[512,512]{1,0:T(8,128)(2,1)}, u32[]{:S(2)}, u32[]{:S(2)}) %collective-permute-start.19) | collective-permute-done | bytes 524320 | tf_op jit(solution)/shard_map/ppermute | solution.py:75
  252.1 11.1 %fusion.82 = f32[512,2816]{1,0:T(8,128)} fusion(bf16[512,2048]{1,0:T(8,128)(2,1)S(1)} %fusion.24, bf16[2048,2816]{1,0:T(8,128)(2,1)} %all-gather.10.cloned.1.call-done), kind=kOutput, calls=%fused_computation.254 | convolution fusion | flops 5905580032 | bytes 19398656 | tf_op jit(solution)/shard_map/dot_general | solution.py:45
  263.2 9.5 %multiply_convert_fusion.1 = (bf16[512,1408]{1,0:T(8,128)(2,1)S(1)}, bf16[512,1408]{1,0:T(8,128)(2,1)S(1)}, bf16[512,1408]{1,0:T(8,128)(2,1)S(1)}) fusion(f32[512,2816]{1,0:T(8,128)} %fusion.82, bf16[1408,2048]{1,0:T(8,128)(2,1)} %all-gather.12.cloned.1.call-done, bf16[512,512]{1,0:T(8,128)(2,1)} %copy-done.34, bf16[512,512]{1,0:T(8,128)(2,1)} %copy-done.35, ...), kind=kOutput, calls=%fused_computation.50 | convolution fusion | flops 2972712960 | bytes 17956864 | tf_op jit(solution)/shard_map/dot_general | solution.py:45
  301.7 19.5 %reduce-scatter.4.cloned.1.call-done = bf16[512,512]{1,0:T(8,128)(2,1)} async-done(((bf16[512,2048]{1,0:T(8,128)(2,1)}), bf16[512,512]{1,0:T(8,128)(2,1)}) %reduce-scatter.4.cloned.1.call-update) | async-done | bytes 524304 | tf_op jit(solution)/shard_map/reduce_scatter | solution.py:132
  333.0 7.4 %convolution_convert_fusion.3 = bf16[512,2048]{1,0:T(8,128)(2,1)} fusion(bf16[512,1408]{1,0:T(8,128)(2,1)S(1)} %get-tuple-element.165, bf16[1408,2048]{1,0:T(8,128)(2,1)} %all-gather.12.cloned.1.call-done), kind=kOutput, calls=%fused_computation.48 | convolution fusion | flops 2953838592 | bytes 9306112 | tf_op jit(solution)/shard_map/dot_general | solution.py:45
  341.9 5.6 add_convert_fusion.1
  347.5 20.1 %all-gather.14.cloned.1.call-done = bf16[512,2048]{1,0:T(8,128)(2,1)} async-done(((bf16[512,512]{1,0:T(8,128)(2,1)}), bf16[512,2048]{1,0:T(8,128)(2,1)}) %all-gather.14.cloned.1.call-update) | async-done | bytes 2097168 | tf_op jit(solution)/shard_map/all_gather | solution.py:128
  380.3 9.9 %fusion.32 = f32[2,1280,64]{1,2,0:T(8,128)} fusion(bf16[2,256,8,64]{1,3,2,0:T(8,128)(2,1)S(1)} %copy.56, f32[2,1280,256,8]{2,1,3,0:T(8,128)} %copy-done, f32[2,8,256]{2,1,0:T(8,128)} %copy-done.82, pred[2,256,1280]{1,2,0:T(8,128)(4,1)S(1)} %bitcast.247), kind=kOutput, calls=%fused_computation.56 | convolution fusion | flops 692060160 | bytes 22822912 | tf_op jit(solution)/shard_map/bhlm,blhd->bmd/dot_general | solution.py:200
  390.2 11.2 %fusion.2 = bf16[2,8,256,1280]{2,3,1,0:T(8,128)(2,1)S(1)} fusion(f32[2,1280,256,8]{2,1,3,0:T(8,128)} %copy-done, bf16[2,256,8,64]{1,3,2,0:T(8,128)(2,1)} %copy-done.45, f32[2,8,256]{2,1,0:T(8,128)S(1)} %bitcast.264, f32[2,8,256]{2,1,0:T(8,128)S(1)} %copy-done.83, pred[2,256,1280]{1,2,0:T(8,128)(4,1)} %bitcast.246, bf16[2,1280,128]{1,2,0:T(8,128)(2,1)} %copy-done.60), kind=kOutput, calls=%fused_computation.3 | convolution fusion | flops 707788800 | bytes 32997376 | tf_op jit(solution)/shard_map/blhd,bmd->bhlm/dot_general | solution.py:201
  425.8 5.4 multiply_reduce_fusion.1
  462.3 15.3 %collective-permute-done.33 = bf16[256,640]{1,0:T(8,128)(2,1)} collective-permute-done((bf16[256,640]{1,0:T(8,128)(2,1)}, bf16[256,640]{1,0:T(8,128)(2,1)}, u32[]{:S(2)}, u32[]{:S(2)}) %collective-permute-start.33) | collective-permute-done | bytes 327712 | tf_op jit(solution)/shard_map/ppermute | solution.py:57
  483.6 17.1 %collective-permute-done.40 = bf16[256,1408]{1,0:T(8,128)(2,1)S(1)} collective-permute-done((bf16[256,1408]{1,0:T(8,128)(2,1)}, bf16[256,1408]{1,0:T(8,128)(2,1)S(1)}, u32[]{:S(2)}, u32[]{:S(2)}) %collective-permute-start.40) | collective-permute-done | bytes 720928 | tf_op jit(solution)/shard_map/ppermute | solution.py:57
  510.9 22.9 %collective-permute-done.43 = bf16[256,1408]{1,0:T(8,128)(2,1)} collective-permute-done((bf16[256,1408]{1,0:T(8,128)(2,1)}, bf16[256,1408]{1,0:T(8,128)(2,1)}, u32[]{:S(2)}, u32[]{:S(2)}) %collective-permute-start.43) | collective-permute-done | bytes 720928 | tf_op jit(solution)/shard_map/ppermute | solution.py:57
  537.3 30.9 %collective-permute-done.47 = bf16[1408,256]{1,0:T(8,128)(2,1)} collective-permute-done((bf16[1408,256]{1,0:T(8,128)(2,1)}, bf16[1408,256]{1,0:T(8,128)(2,1)}, u32[]{:S(2)}, u32[]{:S(2)}) %collective-permute-start.47) | collective-permute-done | bytes 720928 | tf_op jit(solution)/shard_map/ppermute | solution.py:57
  (430 shorter events, 241.2 us)
Async XLA Ops:
  7.2 40.3 %all-gather.6.cloned.1.call-start = ((), (), s32[]{:S(2)}) async-start(), calls=%async_computation.3 | async-start | bytes 3538944 | tf_op jit(solution)/shard_map/all_gather | solution.py:243
  12.4 135.3 %all-gather.8.cloned.1.call-start = ((), (), s32[]{:S(2)}) async-start(), calls=%async_computation.4 | async-start | bytes 2359296 | tf_op jit(solution)/shard_map/all_gather | solution.py:259
  69.1 183.0 %all-gather.10.cloned.1.call-start = ((), (), s32[]{:S(2)}) async-start(), calls=%async_computation.5 | async-start | bytes 12976128 | tf_op jit(solution)/shard_map/all_gather | solution.py:260
  69.9 193.3 %all-gather.12.cloned.1.call-start = ((), (), s32[]{:S(2)}) async-start(), calls=%async_computation.6 | async-start | bytes 6488064 | tf_op jit(solution)/shard_map/all_gather | solution.py:263
  92.6 25.3 %collective-permute-start.10 = (bf16[1,512,512]{2,1,0:T(8,128)(2,1)S(1)}, bf16[1,512,512]{2,1,0:T(8,128)(2,1)}, u32[]{:S(2)}, u32[]{:S(2)}) collective-permute-start(bf16[1,512,512]{2,1,0:T(8,128)(2,1)S(1)} %bitcast.260), channel_id=1, source_target_pairs={{0,2},{1,3},{2,0},{3,1},{4,6},{5,7},{6,4},{7,5},{8,10},{9,11},{10,... | collective-permute-start | bytes 1572872 | tf_op jit(solution)/shard_map/ppermute | solution.py:57
  93.1 228.2 %reduce-scatter.4.cloned.1.call-start = ((), (), s32[]{:S(2)}) async-start(), calls=%async_computation.7 | async-start | bytes 2621440 | tf_op jit(solution)/shard_map/reduce_scatter | solution.py:132
  119.1 25.3 %collective-permute-start.11 = (bf16[2,512,512]{2,1,0:T(8,128)(2,1)S(1)}, bf16[2,512,512]{2,1,0:T(8,128)(2,1)}, u32[]{:S(2)}, u32[]{:S(2)}) collective-permute-start(bf16[2,512,512]{2,1,0:T(8,128)(2,1)S(1)} %pad_maximum_fusion.5), channel_id=1, source_target_pairs={{0,1},{1,0},{2,3},{3,2},{4,5},{5,4},{6,7},{7,6},{8,9},{9,8},{10,11... | collective-permute-start | bytes 3145736 | tf_op jit(solution)/shard_map/ppermute | solution.py:57
  280.9 86.6 %all-gather.14.cloned.1.call-start = ((), (), s32[]{:S(2)}) async-start(), calls=%async_computation.8 | async-start | bytes 2621440 | tf_op jit(solution)/shard_map/all_gather | solution.py:128
  292.1 49.8 %collective-permute-start.45 = (bf16[1408,1024]{1,0:T(8,128)(2,1)}, bf16[1408,1024]{1,0:T(8,128)(2,1)}, u32[]{:S(2)}, u32[]{:S(2)}) collective-permute-start(bf16[1408,1024]{1,0:T(8,128)(2,1)} %convolution_convert_fusion), channel_id=1, source_target_pairs={{0,4},{4,0},{8,12},{12,8},{16,20},{20,16},{24,28},{28,24},{1,5},{5... | collective-permute-start | bytes 8650760 | tf_op jit(solution)/shard_map/ppermute | solution.py:57
  321.3 136.3 %reduce-scatter.6.cloned.1.call-start = ((), (), s32[]{:S(2)}) async-start(), calls=%async_computation.9 | async-start | bytes 2621440 | tf_op jit(solution)/shard_map/reduce_scatter | solution.py:132
  340.4 141.6 %collective-permute-start.39 = (bf16[256,1408]{1,0:T(8,128)(2,1)}, bf16[256,1408]{1,0:T(8,128)(2,1)}, u32[]{:S(2)}, u32[]{:S(2)}) collective-permute-start(bf16[256,1408]{1,0:T(8,128)(2,1)} %get-tuple-element.180), channel_id=1, source_target_pairs={{0,8},{4,12},{8,0},{12,4},{16,24},{20,28},{24,16},{28,20},{1,9},{5... | collective-permute-start | bytes 2162696 | tf_op jit(solution)/shard_map/ppermute | solution.py:57
  409.6 170.0 %reduce-scatter.8.cloned.1.call-start = ((), (), s32[]{:S(2)}) async-start(), calls=%async_computation.10 | async-start | bytes 2621440 | tf_op jit(solution)/shard_map/reduce_scatter | solution.py:132
  452.7 24.9 %collective-permute-start.33 = (bf16[256,640]{1,0:T(8,128)(2,1)}, bf16[256,640]{1,0:T(8,128)(2,1)}, u32[]{:S(2)}, u32[]{:S(2)}) collective-permute-start(bf16[256,640]{1,0:T(8,128)(2,1)} %get-tuple-element.226), channel_id=1, source_target_pairs={{0,16},{4,20},{8,24},{12,28},{16,0},{20,4},{24,8},{28,12},{1,17},{... | collective-permute-start | bytes 983048 | tf_op jit(solution)/shard_map/ppermute | solution.py:57
  457.6 46.6 %collective-permute-start.35 = (bf16[512,1024]{1,0:T(8,128)(2,1)}, bf16[512,1024]{1,0:T(8,128)(2,1)S(1)}, u32[]{:S(2)}, u32[]{:S(2)}) collective-permute-start(bf16[512,1024]{1,0:T(8,128)(2,1)} %convolution_convert_fusion.5), channel_id=1, source_target_pairs={{0,4},{4,0},{8,12},{12,8},{16,20},{20,16},{24,28},{28,24},{1,5},{5... | collective-permute-start | bytes 3145736 | tf_op jit(solution)/shard_map/ppermute | solution.py:57
  462.2 38.5 %collective-permute-start.40 = (bf16[256,1408]{1,0:T(8,128)(2,1)}, bf16[256,1408]{1,0:T(8,128)(2,1)S(1)}, u32[]{:S(2)}, u32[]{:S(2)}) collective-permute-start(bf16[256,1408]{1,0:T(8,128)(2,1)} %get-tuple-element.179), channel_id=1, source_target_pairs={{0,16},{4,20},{8,24},{12,28},{16,0},{20,4},{24,8},{28,12},{1,17},{... | collective-permute-start | bytes 2162696 | tf_op jit(solution)/shard_map/ppermute | solution.py:57
  477.6 25.0 %collective-permute-start.42 = (bf16[256,1408]{1,0:T(8,128)(2,1)}, bf16[256,1408]{1,0:T(8,128)(2,1)S(1)}, u32[]{:S(2)}, u32[]{:S(2)}) collective-permute-start(bf16[256,1408]{1,0:T(8,128)(2,1)} %get-tuple-element.176), channel_id=1, source_target_pairs={{0,8},{4,12},{8,0},{12,4},{16,24},{20,28},{24,16},{28,20},{1,9},{5... | collective-permute-start | bytes 2162696 | tf_op jit(solution)/shard_map/ppermute | solution.py:57
  482.0 51.8 %collective-permute-start.43 = (bf16[256,1408]{1,0:T(8,128)(2,1)}, bf16[256,1408]{1,0:T(8,128)(2,1)}, u32[]{:S(2)}, u32[]{:S(2)}) collective-permute-start(bf16[256,1408]{1,0:T(8,128)(2,1)} %get-tuple-element.175), channel_id=1, source_target_pairs={{0,16},{4,20},{8,24},{12,28},{16,0},{20,4},{24,8},{28,12},{1,17},{... | collective-permute-start | bytes 2162696 | tf_op jit(solution)/shard_map/ppermute | solution.py:57
  500.7 33.1 %collective-permute-start.44 = (bf16[256,1408]{1,0:T(8,128)(2,1)}, bf16[256,1408]{1,0:T(8,128)(2,1)}, u32[]{:S(2)}, u32[]{:S(2)}) collective-permute-start(bf16[256,1408]{1,0:T(8,128)(2,1)} %get-tuple-element.174), channel_id=1, source_target_pairs={{0,24},{4,28},{8,16},{12,20},{16,8},{20,12},{24,0},{28,4},{1,25},{... | collective-permute-start | bytes 2162696 | tf_op jit(solution)/shard_map/ppermute | solution.py:57
  500.7 34.6 %collective-permute-start.46 = (bf16[1408,256]{1,0:T(8,128)(2,1)}, bf16[1408,256]{1,0:T(8,128)(2,1)}, u32[]{:S(2)}, u32[]{:S(2)}) collective-permute-start(bf16[1408,256]{1,0:T(8,128)(2,1)} %get-tuple-element.171), channel_id=1, source_target_pairs={{0,8},{4,12},{8,0},{12,4},{16,24},{20,28},{24,16},{28,20},{1,9},{5... | collective-permute-start | bytes 2162696 | tf_op jit(solution)/shard_map/ppermute | solution.py:57
  502.6 65.6 %collective-permute-start.47 = (bf16[1408,256]{1,0:T(8,128)(2,1)}, bf16[1408,256]{1,0:T(8,128)(2,1)}, u32[]{:S(2)}, u32[]{:S(2)}) collective-permute-start(bf16[1408,256]{1,0:T(8,128)(2,1)} %get-tuple-element.170), channel_id=1, source_target_pairs={{0,16},{4,20},{8,24},{12,28},{16,0},{20,4},{24,8},{28,12},{1,17},{... | collective-permute-start | bytes 2162696 | tf_op jit(solution)/shard_map/ppermute | solution.py:57
  505.2 63.0 %collective-permute-start.48 = (bf16[1408,256]{1,0:T(8,128)(2,1)}, bf16[1408,256]{1,0:T(8,128)(2,1)}, u32[]{:S(2)}, u32[]{:S(2)}) collective-permute-start(bf16[1408,256]{1,0:T(8,128)(2,1)} %get-tuple-element.169), channel_id=1, source_target_pairs={{0,24},{4,28},{8,16},{12,20},{16,8},{20,12},{24,0},{28,4},{1,25},{... | collective-permute-start | bytes 2162696 | tf_op jit(solution)/shard_map/ppermute | solution.py:57
  533.8 43.5 %collective-permute-start.36 = (bf16[512,256]{1,0:T(8,128)(2,1)S(1)}, bf16[512,256]{1,0:T(8,128)(2,1)S(1)}, u32[]{:S(2)}, u32[]{:S(2)}) collective-permute-start(bf16[512,256]{1,0:T(8,128)(2,1)S(1)} %get-tuple-element.231), channel_id=1, source_target_pairs={{0,8},{4,12},{8,0},{12,4},{16,24},{20,28},{24,16},{28,20},{1,9},{5... | collective-permute-start | bytes 786440 | tf_op jit(solution)/shard_map/ppermute | solution.py:57
  533.8 43.5 %collective-permute-start.37 = (bf16[512,256]{1,0:T(8,128)(2,1)S(1)}, bf16[512,256]{1,0:T(8,128)(2,1)S(1)}, u32[]{:S(2)}, u32[]{:S(2)}) collective-permute-start(bf16[512,256]{1,0:T(8,128)(2,1)S(1)} %get-tuple-element.230), channel_id=1, source_target_pairs={{0,16},{4,20},{8,24},{12,28},{16,0},{20,4},{24,8},{28,12},{1,17},{... | collective-permute-start | bytes 786440 | tf_op jit(solution)/shard_map/ppermute | solution.py:57
  535.3 42.0 %collective-permute-start.38 = (bf16[512,256]{1,0:T(8,128)(2,1)S(1)}, bf16[512,256]{1,0:T(8,128)(2,1)S(1)}, u32[]{:S(2)}, u32[]{:S(2)}) collective-permute-start(bf16[512,256]{1,0:T(8,128)(2,1)S(1)} %get-tuple-element.229), channel_id=1, source_target_pairs={{0,24},{4,28},{8,16},{12,20},{16,8},{20,12},{24,0},{28,4},{1,25},{... | collective-permute-start | bytes 786440 | tf_op jit(solution)/shard_map/ppermute | solution.py:57
  (122 other events, 1601.3 us)
Sparse Core Ops, SparseCore 0:
  12.5 34.9 all-gather.5
  69.3 31.9 all-gather.7
  103.7 67.5 all-gather.9
  173.1 44.2 all-gather.11
  281.1 40.1 reduce-scatter.3
  322.7 44.8 all-gather.13
  409.8 42.9 reduce-scatter.5
  457.7 42.2 reduce-scatter.7

commit v2 on v1

--- a/solution.py
+++ b/solution.py
@@ -104,7 +104,7 @@
     return jnp.concatenate(held, 1)
 
 
-def tp_scatter_sum(partial):
+def tp_scatter_sum(partial, *late):
     size = lax.axis_size("tp")
     index = lax.axis_index("tp")
     width = partial.shape[1] // size
@@ -116,6 +116,8 @@
             [jnp.where(low, b, a).astype(BF16) for a, b in zip(held[0::2], held[1::2])]
         )
         other = exchange(send, "tp", bit)
+        if late and 2 * bit >= size:
+            other = after(other, *late)
         held = [
             jnp.where(low, a, b) + other[slot].astype(F32)
             for slot, (a, b) in enumerate(zip(held[0::2], held[1::2]))
@@ -187,19 +189,22 @@
     return (heads.astype(BF16), log_total)
 
 
-def attend_backward(
-    query_rotated, keys, values, allowed, log_total, heads_low, grad_low, score_scale
-):
-    delta = jnp.swapaxes(jnp.sum(grad_low.astype(F32) * heads_low.astype(F32), -1), 1, 2)
+def attention_weights(query_rotated, keys, allowed, log_total, score_scale):
     scores = (
         jnp.einsum("blhd,bmd->bhlm", query_rotated, keys, preferred_element_type=F32)
         * score_scale
     )
-    prob_exact = jnp.where(allowed, jnp.exp(scores - log_total[..., None]), 0.0)
-    prob_round = prob_exact.astype(BF16)
-    grad_values = jnp.einsum("bhlm,blhd->bmd", prob_round, grad_low, preferred_element_type=F32)
+    weights = jnp.where(allowed, jnp.exp(scores - log_total[..., None]), 0.0).astype(BF16)
+    return lax.optimization_barrier(weights)
+
+
+def attend_backward(query_rotated, keys, values, weights, heads_low, grad_low, score_scale):
+    delta = jnp.swapaxes(jnp.sum(grad_low.astype(F32) * heads_low.astype(F32), -1), 1, 2)
+    grad_values = jnp.einsum("bhlm,blhd->bmd", weights, grad_low, preferred_element_type=F32)
     grad_probs = jnp.einsum("blhd,bmd->bhlm", grad_low, values, preferred_element_type=F32)
-    grad_scores = (prob_exact * (grad_probs - delta[..., None]) * score_scale).astype(BF16)
+    grad_scores = (
+        weights.astype(F32) * (grad_probs - delta[..., None]) * score_scale
+    ).astype(BF16)
     grad_query = jnp.einsum("bhlm,bmd->blhd", grad_scores, keys, preferred_element_type=F32)
     grad_keys = jnp.einsum(
         "bhlm,blhd->bmd", grad_scores, query_rotated, preferred_element_type=F32
@@ -313,6 +318,9 @@
     grads_order = owner_order(grad_in)
     down_terms, _ = owner_terms(grads_order, lambda block: dot_tn(activated, block), 1)
     grad_normed_two = queue_gather(after(partial_two, *gate_sent, *up_sent))
+    weights = attention_weights(
+        after(query_rotated, grad_up_low), keys, allowed, totals, score_scale
+    )
     mlp_partial = dot_nn(activated, down_weight).astype(BF16)
     mlp_own = queue_scatter_sum(after(mlp_partial, grad_normed_two))
     output = (middle_own + mlp_own.astype(F32)).astype(BF16)
@@ -333,7 +341,7 @@
         dot_nt(middle_low, out_weight).astype(BF16).reshape(rows, head_count, HEAD_SIZE)
     )
     grad_query_rot, grad_keys, grad_values = attend_backward(
-        query_rotated, keys, values, allowed, totals, heads, grad_heads, score_scale
+        query_rotated, keys, values, weights, heads, grad_heads, score_scale
     )
     grad_window = jnp.concatenate([grad_keys, grad_values], -1)
     own_pairs = grad_window[:, back * row_count :]
@@ -349,10 +357,17 @@
     grad_projected = lax.optimization_barrier(
         jnp.concatenate([grad_query_low, grad_key_low, grad_value_low], 1)
     )
+    normed_one_order = owner_order(normed_one)
+    project_terms, project_sent = owner_terms(
+        normed_one_order, lambda block: dot_tn(block, grad_projected), 0
+    )
     grad_one = dot_nt(grad_projected, project_weight)
     weighted = grad_one * inputs
     norm_sum_one = jnp.sum(weighted * scale_one, 0)
-    summed = queue_scatter_sum(after(grad_one.astype(BF16), mlp_own))
+    summed = by_batch(after(grad_one.astype(BF16), mlp_own))
+    summed = [queue_scatter_sum(summed[0]), summed[1:].reshape(rows - row_count, full_width)]
+    summed[1] = tp_scatter_sum(summed[1].astype(F32), *project_sent)
+    summed = jnp.concatenate([block.astype(F32) for block in summed])
     small = jnp.concatenate([norm_sum_one, jnp.sum(weighted * gain_one, -1) / full_width])
     for bit in range((lax.axis_size("tp") - 1).bit_length()):
         small = small + exchange(small, "tp", 1 << bit)
@@ -363,22 +378,18 @@
     grad_middle_own = lax.dynamic_slice_in_dim(grad_middle, column_start, local_width, 1)
     input_grad = (
         grad_middle_own
-        + scale_one * (summed.astype(F32) * gain_one_own)
+        + scale_one * (summed * gain_one_own)
         - tokens_own.astype(F32) * (scale_one * scale_one * scale_one) * row_mean
     )
-    normed_one_order = owner_order(normed_one)
-    project_terms, project_sent = owner_terms(
-        normed_one_order, lambda block: dot_tn(block, grad_projected), 0
-    )
     middle_order = owner_order(after(middle_low, *project_sent))
-    out_terms, out_sent = owner_terms(middle_order, lambda block: dot_tn(heads_out, block), 1)
+    out_terms, _ = owner_terms(middle_order, lambda block: dot_tn(heads_out, block), 1)
     grad_scale = (batch_count * row_count * lax.axis_size("fsdp")) ** (-0.5)
     norm_start = lax.axis_index("fsdp") * shard_rows
     norm_sums = norm_sums * grad_scale
-    down_sum = owner_total(down_terms, *out_sent)
-    gate_sum = owner_total(gate_terms, *out_sent)
-    up_sum = owner_total(up_terms, *out_sent)
-    out_sum = owner_total(out_terms, *out_sent)
+    down_sum = owner_total(down_terms, *project_sent)
+    gate_sum = owner_total(gate_terms, *project_sent)
+    up_sum = owner_total(up_terms, *project_sent)
+    out_sum = owner_total(out_terms)
     project_sum = owner_total(project_terms) * grad_scale
     return (
         by_batch(output),

time: 598 us -> 625 us (1.045)
  waiting for transfers between devices: 294 us -> 306 us
    ppermute x29 -> x31, waiting for transfers between devices: 177 us -> 188 us  [exchange(): lax.ppermute(block, axis, [(i, i ^ mask) for i in range(lax.axis_size(axi...]
    dot_general x1 -> x2, matrix products: 9.93 us -> 15.9 us  [the longest x1 8.07 us: attend_backward(): jnp.einsum('bhlm,blhd->bmd', weights, grad_low, preferred_element_type=F32)]
    ppermute x29 -> x31, starting transfers between devices: 24.1 us -> 27.9 us  [exchange(): lax.ppermute(block, axis, [(i, i ^ mask) for i in range(lax.axis_size(axi...]
    unnamed x188 -> x190, local copies, waits for them, and re-layouts: 14.4 us -> 17.1 us
  transfers between devices with their start and end apart: 57 -> 59, of which waited for: 26 -> 28; matrix products, arithmetic and copies ran while one was open for 31% -> 31% of each run, Pallas kernels for 0% -> 0%
where the time goes in v2:
time: 625 us; the launch traced here: 616 us
  waiting for transfers between devices  306 us (49%)
  matrix products  127 us (20%)
  starting transfers between devices  63 us (10%)
  other arithmetic  61.5 us (10%)
  local copies, waits for them, and re-layouts  41.6 us (7%)
  between operations  16.1 us (3%)
    ppermute x31, waiting for transfers between devices, exchange(): lax.ppermute(block, axis, [(i, i ^ mask) for i in range(lax.axis_size(axi...  188 us
    ppermute x6, waiting for transfers between devices, tp_gather(): lax.ppermute(upper, 'tp', [(i, i - 1) for i in range(1, size - step + 1)])  47 us
    dot_general x25, matrix products, dot_tn(): lax.dot_general(left, right, (((0,), (0,)), ((), ())), preferred_element_...  38.5 us
    dot_general x5, matrix products, dot_nn(): return jnp.dot(left, right, preferred_element_type=F32)  33.9 us
    ppermute x31, starting transfers between devices, exchange(): lax.ppermute(block, axis, [(i, i ^ mask) for i in range(lax.axis_size(axi...  27.9 us
    reduce_scatter x3, waiting for transfers between devices, queue_scatter_sum(): lax.psum_scatter(partial.astype(BF16), 'tp', scatter_dimension=1, tiled=T...  24.3 us
    unnamed x190, local copies, waits for them, and re-layouts  17.1 us
    ppermute x8, starting transfers between devices, passed_along(): return lax.ppermute(block, axis, route)  16.2 us
  transfers between devices with their start and end apart: 59, of which 28 were waited for; matrix products, arithmetic and copies ran while one was open for 31% of the time, Pallas kernels for 0%

profile of v2, /device:TPU:0, one launch (start us, length us, event | category | flops | bytes accessed | tf_op | source)
XLA Modules:
  0.0 615.7 jit_solution(5314399810677142132)
XLA Ops:
  35.8 11.7 %all-gather.6.cloned.1.call-done = bf16[2048,768]{1,0:T(8,128)(2,1)} async-done(((bf16[256,768]{1,0:T(8,128)(2,1)}), bf16[2048,768]{1,0:T(8,128)(2,1)}) %all-gather.6.cloned.1.call-update) | async-done | bytes 3145744 | tf_op jit(solution)/shard_map/all_gather | solution.py:248
  52.7 13.5 %collective-permute-done.5 = bf16[512,512]{1,0:T(8,128)(2,1)} collective-permute-done((bf16[512,512]{1,0:T(8,128)(2,1)S(1)}, bf16[512,512]{1,0:T(8,128)(2,1)}, u32[]{:S(2)}, u32[]{:S(2)}) %collective-permute-start.5) | collective-permute-done | bytes 524320 | tf_op jit(solution)/shard_map/ppermute | solution.py:75
  107.8 10.0 %collective-permute-done.10 = bf16[1,512,512]{2,1,0:T(8,128)(2,1)} collective-permute-done((bf16[1,512,512]{2,1,0:T(8,128)(2,1)S(1)}, bf16[1,512,512]{2,1,0:T(8,128)(2,1)}, u32[]{:S(2)}, u32[]{:S(2)}) %collective-permute-start.10) | collective-permute-done | bytes 524320 | tf_op jit(solution)/shard_map/ppermute | solution.py:57
  125.4 19.0 %collective-permute-done.11 = bf16[2,512,512]{2,1,0:T(8,128)(2,1)} collective-permute-done((bf16[2,512,512]{2,1,0:T(8,128)(2,1)S(1)}, bf16[2,512,512]{2,1,0:T(8,128)(2,1)}, u32[]{:S(2)}, u32[]{:S(2)}) %collective-permute-start.11) | collective-permute-done | bytes 1048608 | tf_op jit(solution)/shard_map/ppermute | solution.py:57
  151.4 23.8 %collective-permute-done.12 = bf16[2,512,512]{2,1,0:T(8,128)(2,1)S(1)} collective-permute-done((bf16[2,512,512]{2,1,0:T(8,128)(2,1)S(1)}, bf16[2,512,512]{2,1,0:T(8,128)(2,1)S(1)}, u32[]{:S(2)}, u32[]{:S(2)}) %collective-permute-start.12) | collective-permute-done | bytes 1048608 | tf_op jit(solution)/shard_map/ppermute | solution.py:57
  176.6 23.6 %collective-permute-done.13 = bf16[1,512,512]{2,1,0:T(8,128)(2,1)S(1)} collective-permute-done((bf16[1,512,512]{2,1,0:T(8,128)(2,1)S(1)}, bf16[1,512,512]{2,1,0:T(8,128)(2,1)S(1)}, u32[]{:S(2)}, u32[]{:S(2)}) %collective-permute-start.13) | collective-permute-done | bytes 524320 | tf_op jit(solution)/shard_map/ppermute | solution.py:57
  204.5 9.9 %collective-permute-done.14 = bf16[512,512]{1,0:T(8,128)(2,1)S(1)} collective-permute-done((bf16[512,512]{1,0:T(8,128)(2,1)S(1)}, bf16[512,512]{1,0:T(8,128)(2,1)S(1)}, u32[]{:S(2)}, u32[]{:S(2)}) %collective-permute-start.14) | collective-permute-done | bytes 524320 | tf_op jit(solution)/shard_map/ppermute | solution.py:74
  220.6 12.5 %collective-permute-done.18 = bf16[512,512]{1,0:T(8,128)(2,1)S(1)} collective-permute-done((bf16[512,512]{1,0:T(8,128)(2,1)S(1)}, bf16[512,512]{1,0:T(8,128)(2,1)S(1)}, u32[]{:S(2)}, u32[]{:S(2)}) %collective-permute-start.18) | collective-permute-done | bytes 524320 | tf_op jit(solution)/shard_map/ppermute | solution.py:75
  235.4 11.4 %collective-permute-done.19 = bf16[512,512]{1,0:T(8,128)(2,1)} collective-permute-done((bf16[512,512]{1,0:T(8,128)(2,1)S(1)}, bf16[512,512]{1,0:T(8,128)(2,1)}, u32[]{:S(2)}, u32[]{:S(2)}) %collective-permute-start.19) | collective-permute-done | bytes 524320 | tf_op jit(solution)/shard_map/ppermute | solution.py:75
  252.7 12.5 %fusion.81 = f32[512,2816]{1,0:T(8,128)} fusion(bf16[512,2048]{1,0:T(8,128)(2,1)} %copy-done.13, bf16[2048,2816]{1,0:T(8,128)(2,1)} %all-gather.10.cloned.1.call-done), kind=kOutput, calls=%fused_computation.268 | convolution fusion | flops 5905580032 | bytes 19398656 | tf_op jit(solution)/shard_map/dot_general | solution.py:45
  265.3 9.5 %multiply_convert_fusion.1 = (bf16[512,1408]{1,0:T(8,128)(2,1)S(1)}, bf16[512,1408]{1,0:T(8,128)(2,1)S(1)}, bf16[512,1408]{1,0:T(8,128)(2,1)S(1)}) fusion(f32[512,2816]{1,0:T(8,128)} %fusion.81, bf16[1408,2048]{1,0:T(8,128)(2,1)} %all-gather.12.cloned.1.call-done, bf16[512,512]{1,0:T(8,128)(2,1)} %copy-done.34, bf16[512,512]{1,0:T(8,128)(2,1)} %copy-done.35, ...), kind=kOutput, calls=%fused_computation.48 | convolution fusion | flops 2972712960 | bytes 17956864 | tf_op jit(solution)/shard_map/dot_general | solution.py:45
  299.1 24.3 %reduce-scatter.4.cloned.1.call-done = bf16[512,512]{1,0:T(8,128)(2,1)} async-done(((bf16[512,2048]{1,0:T(8,128)(2,1)}), bf16[512,512]{1,0:T(8,128)(2,1)}) %reduce-scatter.4.cloned.1.call-update) | async-done | bytes 524304 | tf_op jit(solution)/shard_map/reduce_scatter | solution.py:134
  333.7 7.8 %fusion.5 = bf16[2,8,256,1280]{2,3,1,0:T(8,128)(2,1)} fusion(f32[2,8,256]{2,1,0:T(8,128)S(1)} %log_add_fusion, pred[2,256,1280]{1,2,0:T(8,128)(4,1)S(1)} %bitcast.271, bf16[2,256,8,64]{1,0,3,2:T(2,128)(2,1)S(1)} %copy-done.29, bf16[2,1280,128]{1,2,0:T(8,128)(2,1)S(1)} %copy-done.59), kind=kOutput, calls=%fused_computation.7 | convolution fusion | flops 692060160 | bytes 12009472 | tf_op jit(solution)/shard_map/blhd,bmd->bhlm/dot_general | solution.py:194
  346.5 7.2 %convolution_convert_fusion.3 = bf16[512,2048]{1,0:T(8,128)(2,1)} fusion(bf16[512,1408]{1,0:T(8,128)(2,1)S(1)} %get-tuple-element.169, bf16[1408,2048]{1,0:T(8,128)(2,1)} %all-gather.12.cloned.1.call-done), kind=kOutput, calls=%fused_computation.46 | convolution fusion | flops 2953838592 | bytes 9306112 | tf_op jit(solution)/shard_map/dot_general | solution.py:45
  353.8 15.9 %all-gather.14.cloned.1.call-done = bf16[512,2048]{1,0:T(8,128)(2,1)} async-done(((bf16[512,512]{1,0:T(8,128)(2,1)}), bf16[512,2048]{1,0:T(8,128)(2,1)}) %all-gather.14.cloned.1.call-update) | async-done | bytes 2097168 | tf_op jit(solution)/shard_map/all_gather | solution.py:130
  384.1 8.1 %convolution_bitcast_fusion = f32[2,1280,64]{1,2,0:T(8,128)} fusion(bf16[2,8,256,1280]{2,3,1,0:T(8,128)(2,1)} %fusion.5, bf16[2,256,8,64]{1,3,2,0:T(8,128)(2,1)S(1)} %copy.57), kind=kOutput, calls=%fused_computation.53 | convolution fusion | flops 671088640 | bytes 11665408 | tf_op jit(solution)/shard_map/bhlm,blhd->bmd/dot_general | solution.py:203
  392.2 6.4 %fusion.2 = bf16[2,8,256,1280]{2,3,1,0:T(8,128)(2,1)S(1)} fusion(bf16[2,8,256,1280]{2,3,1,0:T(8,128)(2,1)} %fusion.5, bf16[2,256,8,64]{1,3,2,0:T(8,128)(2,1)S(1)} %copy.57, f32[2,8,256]{2,1,0:T(8,128)S(1)} %bitcast.288, bf16[2,1280,128]{1,2,0:T(8,128)(2,1)} %copy-done.58), kind=kOutput, calls=%fused_computation.3 | convolution fusion | flops 697303040 | bytes 21839872 | tf_op jit(solution)/shard_map/blhd,bmd->bhlm/dot_general | solution.py:204
  447.2 21.7 %collective-permute-done.32 = f32[4096]{0:T(1024)S(1)} collective-permute-done((f32[4096]{0:T(1024)S(1)}, f32[4096]{0:T(1024)S(1)}, u32[]{:S(2)}, u32[]{:S(2)}) %collective-permute-start.32) | collective-permute-done | bytes 16416 | tf_op jit(solution)/shard_map/ppermute | solution.py:57
  479.6 12.4 %collective-permute-done.44 = bf16[256,1408]{1,0:T(8,128)(2,1)S(1)} collective-permute-done((bf16[256,1408]{1,0:T(8,128)(2,1)}, bf16[256,1408]{1,0:T(8,128)(2,1)S(1)}, u32[]{:S(2)}, u32[]{:S(2)}) %collective-permute-start.44) | collective-permute-done | bytes 720928 | tf_op jit(solution)/shard_map/ppermute | solution.py:57
  498.4 11.5 %collective-permute-done.45 = bf16[256,1408]{1,0:T(8,128)(2,1)S(1)} collective-permute-done((bf16[256,1408]{1,0:T(8,128)(2,1)S(1)}, bf16[256,1408]{1,0:T(8,128)(2,1)S(1)}, u32[]{:S(2)}, u32[]{:S(2)}) %collective-permute-start.45) | collective-permute-done | bytes 720928 | tf_op jit(solution)/shard_map/ppermute | solution.py:57
  511.6 11.3 %collective-permute-done.48 = bf16[1408,256]{1,0:T(8,128)(2,1)S(1)} collective-permute-done((bf16[1408,256]{1,0:T(8,128)(2,1)S(1)}, bf16[1408,256]{1,0:T(8,128)(2,1)S(1)}, u32[]{:S(2)}, u32[]{:S(2)}) %collective-permute-start.48) | collective-permute-done | bytes 720928 | tf_op jit(solution)/shard_map/ppermute | solution.py:57
  524.1 16.7 %collective-permute-done.49 = bf16[1408,256]{1,0:T(8,128)(2,1)S(1)} collective-permute-done((bf16[1408,256]{1,0:T(8,128)(2,1)S(1)}, bf16[1408,256]{1,0:T(8,128)(2,1)S(1)}, u32[]{:S(2)}, u32[]{:S(2)}) %collective-permute-start.49) | collective-permute-done | bytes 720928 | tf_op jit(solution)/shard_map/ppermute | solution.py:57
  574.5 14.8 %collective-permute-done.26 = bf16[2,256,512]{2,1,0:T(8,128)(2,1)S(1)} collective-permute-done((bf16[2,256,512]{2,1,0:T(8,128)(2,1)}, bf16[2,256,512]{2,1,0:T(8,128)(2,1)S(1)}, u32[]{:S(2)}, u32[]{:S(2)}) %collective-permute-start.26) | collective-permute-done | bytes 524320 | tf_op jit(solution)/shard_map/ppermute | solution.py:57
  592.2 11.4 %collective-permute-done.27 = bf16[1,256,512]{2,1,0:T(8,128)(2,1)S(1)} collective-permute-done((bf16[1,256,512]{2,1,0:T(8,128)(2,1)S(1)}, bf16[1,256,512]{2,1,0:T(8,128)(2,1)S(1)}, u32[]{:S(2)}, u32[]{:S(2)}) %collective-permute-start.27) | collective-permute-done | bytes 262176 | tf_op jit(solution)/shard_map/ppermute | solution.py:57
  (443 shorter events, 272.7 us)
Async XLA Ops:
  7.2 40.3 %all-gather.6.cloned.1.call-start = ((), (), s32[]{:S(2)}) async-start(), calls=%async_computation.3 | async-start | bytes 3538944 | tf_op jit(solution)/shard_map/all_gather | solution.py:248
  12.4 135.3 %all-gather.8.cloned.1.call-start = ((), (), s32[]{:S(2)}) async-start(), calls=%async_computation.4 | async-start | bytes 2359296 | tf_op jit(solution)/shard_map/all_gather | solution.py:264
  69.1 183.6 %all-gather.10.cloned.1.call-start = ((), (), s32[]{:S(2)}) async-start(), calls=%async_computation.5 | async-start | bytes 12976128 | tf_op jit(solution)/shard_map/all_gather | solution.py:265
  69.8 195.4 %all-gather.12.cloned.1.call-start = ((), (), s32[]{:S(2)}) async-start(), calls=%async_computation.6 | async-start | bytes 6488064 | tf_op jit(solution)/shard_map/all_gather | solution.py:268
  92.6 25.3 %collective-permute-start.10 = (bf16[1,512,512]{2,1,0:T(8,128)(2,1)S(1)}, bf16[1,512,512]{2,1,0:T(8,128)(2,1)}, u32[]{:S(2)}, u32[]{:S(2)}) collective-permute-start(bf16[1,512,512]{2,1,0:T(8,128)(2,1)S(1)} %bitcast.284), channel_id=1, source_target_pairs={{0,2},{1,3},{2,0},{3,1},{4,6},{5,7},{6,4},{7,5},{8,10},{9,11},{10,... | collective-permute-start | bytes 1572872 | tf_op jit(solution)/shard_map/ppermute | solution.py:57
  93.1 230.2 %reduce-scatter.4.cloned.1.call-start = ((), (), s32[]{:S(2)}) async-start(), calls=%async_computation.7 | async-start | bytes 2621440 | tf_op jit(solution)/shard_map/reduce_scatter | solution.py:134
  119.1 25.3 %collective-permute-start.11 = (bf16[2,512,512]{2,1,0:T(8,128)(2,1)S(1)}, bf16[2,512,512]{2,1,0:T(8,128)(2,1)}, u32[]{:S(2)}, u32[]{:S(2)}) collective-permute-start(bf16[2,512,512]{2,1,0:T(8,128)(2,1)S(1)} %pad_maximum_fusion.5), channel_id=1, source_target_pairs={{0,1},{1,0},{2,3},{3,2},{4,5},{5,4},{6,7},{7,6},{8,9},{9,8},{10,11... | collective-permute-start | bytes 3145736 | tf_op jit(solution)/shard_map/ppermute | solution.py:57
  283.0 86.7 %all-gather.14.cloned.1.call-start = ((), (), s32[]{:S(2)}) async-start(), calls=%async_computation.8 | async-start | bytes 2621440 | tf_op jit(solution)/shard_map/all_gather | solution.py:130
  323.4 230.4 %reduce-scatter.6.cloned.1.call-start = ((), (), s32[]{:S(2)}) async-start(), calls=%async_computation.9 | async-start | bytes 2621440 | tf_op jit(solution)/shard_map/reduce_scatter | solution.py:134
  344.9 95.8 %collective-permute-start.47 = (bf16[1408,1024]{1,0:T(8,128)(2,1)}, bf16[1408,1024]{1,0:T(8,128)(2,1)}, u32[]{:S(2)}, u32[]{:S(2)}) collective-permute-start(bf16[1408,1024]{1,0:T(8,128)(2,1)} %convolution_convert_fusion), channel_id=1, source_target_pairs={{0,4},{4,0},{8,12},{12,8},{16,20},{20,16},{24,28},{28,24},{1,5},{5... | collective-permute-start | bytes 8650760 | tf_op jit(solution)/shard_map/ppermute | solution.py:57
  433.5 41.9 %collective-permute-start.41 = (bf16[256,1408]{1,0:T(8,128)(2,1)}, bf16[256,1408]{1,0:T(8,128)(2,1)}, u32[]{:S(2)}, u32[]{:S(2)}) collective-permute-start(bf16[256,1408]{1,0:T(8,128)(2,1)} %get-tuple-element.184), channel_id=1, source_target_pairs={{0,8},{4,12},{8,0},{12,4},{16,24},{20,28},{24,16},{28,20},{1,9},{5... | collective-permute-start | bytes 2162696 | tf_op jit(solution)/shard_map/ppermute | solution.py:57
  436.4 39.1 %collective-permute-start.42 = (bf16[256,1408]{1,0:T(8,128)(2,1)}, bf16[256,1408]{1,0:T(8,128)(2,1)}, u32[]{:S(2)}, u32[]{:S(2)}) collective-permute-start(bf16[256,1408]{1,0:T(8,128)(2,1)} %get-tuple-element.183), channel_id=1, source_target_pairs={{0,16},{4,20},{8,24},{12,28},{16,0},{20,4},{24,8},{28,12},{1,17},{... | collective-permute-start | bytes 2162696 | tf_op jit(solution)/shard_map/ppermute | solution.py:57
  437.8 40.1 %collective-permute-start.43 = (bf16[256,1408]{1,0:T(8,128)(2,1)}, bf16[256,1408]{1,0:T(8,128)(2,1)}, u32[]{:S(2)}, u32[]{:S(2)}) collective-permute-start(bf16[256,1408]{1,0:T(8,128)(2,1)} %get-tuple-element.182), channel_id=1, source_target_pairs={{0,24},{4,28},{8,16},{12,20},{16,8},{20,12},{24,0},{28,4},{1,25},{... | collective-permute-start | bytes 2162696 | tf_op jit(solution)/shard_map/ppermute | solution.py:57
  440.2 53.2 %collective-permute-start.28 = (bf16[1024,640]{1,0:T(8,128)(2,1)}, bf16[1024,640]{1,0:T(8,128)(2,1)}, u32[]{:S(2)}, u32[]{:S(2)}) collective-permute-start(bf16[1024,640]{1,0:T(8,128)(2,1)} %convolution_convert_fusion.4), channel_id=1, source_target_pairs={{0,4},{4,0},{8,12},{12,8},{16,20},{20,16},{24,28},{28,24},{1,5},{5... | collective-permute-start | bytes 3932168 | tf_op jit(solution)/shard_map/ppermute | solution.py:57
  440.7 28.3 %collective-permute-start.32 = (f32[4096]{0:T(1024)S(1)}, f32[4096]{0:T(1024)S(1)}, u32[]{:S(2)}, u32[]{:S(2)}) collective-permute-start(f32[4096]{0:T(1024)S(1)} %fusion.70), channel_id=1, source_target_pairs={{0,8},{4,12},{8,0},{12,4},{16,24},{20,28},{24,16},{28,20},{1,9},{5... | collective-permute-start | bytes 49160 | tf_op jit(solution)/shard_map/ppermute | solution.py:57
  447.0 158.1 %reduce-scatter.8.cloned.1.call-start = ((), (), s32[]{:S(2)}) async-start(), calls=%async_computation.10 | async-start | bytes 1310720 | tf_op jit(solution)/shard_map/reduce_scatter | solution.py:134
  475.4 34.5 %collective-permute-start.45 = (bf16[256,1408]{1,0:T(8,128)(2,1)S(1)}, bf16[256,1408]{1,0:T(8,128)(2,1)S(1)}, u32[]{:S(2)}, u32[]{:S(2)}) collective-permute-start(bf16[256,1408]{1,0:T(8,128)(2,1)S(1)} %copy-done.63), channel_id=1, source_target_pairs={{0,16},{4,20},{8,24},{12,28},{16,0},{20,4},{24,8},{28,12},{1,17},{... | collective-permute-start | bytes 2162696 | tf_op jit(solution)/shard_map/ppermute | solution.py:57
  475.5 34.4 %collective-permute-start.46 = (bf16[256,1408]{1,0:T(8,128)(2,1)S(1)}, bf16[256,1408]{1,0:T(8,128)(2,1)S(1)}, u32[]{:S(2)}, u32[]{:S(2)}) collective-permute-start(bf16[256,1408]{1,0:T(8,128)(2,1)S(1)} %copy-done.62), channel_id=1, source_target_pairs={{0,24},{4,28},{8,16},{12,20},{16,8},{20,12},{24,0},{28,4},{1,25},{... | collective-permute-start | bytes 2162696 | tf_op jit(solution)/shard_map/ppermute | solution.py:57
  477.9 45.1 %collective-permute-start.48 = (bf16[1408,256]{1,0:T(8,128)(2,1)S(1)}, bf16[1408,256]{1,0:T(8,128)(2,1)S(1)}, u32[]{:S(2)}, u32[]{:S(2)}) collective-permute-start(bf16[1408,256]{1,0:T(8,128)(2,1)S(1)} %copy-done.66), channel_id=1, source_target_pairs={{0,8},{4,12},{8,0},{12,4},{16,24},{20,28},{24,16},{28,20},{1,9},{5... | collective-permute-start | bytes 2162696 | tf_op jit(solution)/shard_map/ppermute | solution.py:57
  492.0 48.8 %collective-permute-start.49 = (bf16[1408,256]{1,0:T(8,128)(2,1)S(1)}, bf16[1408,256]{1,0:T(8,128)(2,1)S(1)}, u32[]{:S(2)}, u32[]{:S(2)}) collective-permute-start(bf16[1408,256]{1,0:T(8,128)(2,1)S(1)} %copy-done.65), channel_id=1, source_target_pairs={{0,16},{4,20},{8,24},{12,28},{16,0},{20,4},{24,8},{28,12},{1,17},{... | collective-permute-start | bytes 2162696 | tf_op jit(solution)/shard_map/ppermute | solution.py:57
  493.3 47.5 %collective-permute-start.50 = (bf16[1408,256]{1,0:T(8,128)(2,1)S(1)}, bf16[1408,256]{1,0:T(8,128)(2,1)S(1)}, u32[]{:S(2)}, u32[]{:S(2)}) collective-permute-start(bf16[1408,256]{1,0:T(8,128)(2,1)S(1)} %copy-done.64), channel_id=1, source_target_pairs={{0,24},{4,28},{8,16},{12,20},{16,8},{20,12},{24,0},{28,4},{1,25},{... | collective-permute-start | bytes 2162696 | tf_op jit(solution)/shard_map/ppermute | solution.py:57
  509.9 40.2 %collective-permute-start.34 = (bf16[256,640]{1,0:T(8,128)(2,1)S(1)}, bf16[256,640]{1,0:T(8,128)(2,1)S(1)}, u32[]{:S(2)}, u32[]{:S(2)}) collective-permute-start(bf16[256,640]{1,0:T(8,128)(2,1)S(1)} %get-tuple-element.236), channel_id=1, source_target_pairs={{0,8},{4,12},{8,0},{12,4},{16,24},{20,28},{24,16},{28,20},{1,9},{5... | collective-permute-start | bytes 983048 | tf_op jit(solution)/shard_map/ppermute | solution.py:57
  509.9 42.4 %collective-permute-start.35 = (bf16[256,640]{1,0:T(8,128)(2,1)S(1)}, bf16[256,640]{1,0:T(8,128)(2,1)S(1)}, u32[]{:S(2)}, u32[]{:S(2)}) collective-permute-start(bf16[256,640]{1,0:T(8,128)(2,1)S(1)} %get-tuple-element.235), channel_id=1, source_target_pairs={{0,16},{4,20},{8,24},{12,28},{16,0},{20,4},{24,8},{28,12},{1,17},{... | collective-permute-start | bytes 983048 | tf_op jit(solution)/shard_map/ppermute | solution.py:57
  523.0 29.3 %collective-permute-start.36 = (bf16[256,640]{1,0:T(8,128)(2,1)S(1)}, bf16[256,640]{1,0:T(8,128)(2,1)S(1)}, u32[]{:S(2)}, u32[]{:S(2)}) collective-permute-start(bf16[256,640]{1,0:T(8,128)(2,1)S(1)} %get-tuple-element.234), channel_id=1, source_target_pairs={{0,24},{4,28},{8,16},{12,20},{16,8},{20,12},{24,0},{28,4},{1,25},{... | collective-permute-start | bytes 983048 | tf_op jit(solution)/shard_map/ppermute | solution.py:57
  (125 other events, 1362.1 us)
Sparse Core Ops, SparseCore 0:
  12.5 34.8 all-gather.5
  69.2 31.8 all-gather.7
  103.6 67.5 all-gather.9
  172.9 44.2 all-gather.11
  283.1 40.2 reduce-scatter.3
  324.8 44.8 all-gather.13
  447.1 41.9 reduce-scatter.5
  556.7 36.0 reduce-scatter.7

commit v3 on v2

--- a/solution.py
+++ b/solution.py
@@ -364,10 +364,7 @@
     grad_one = dot_nt(grad_projected, project_weight)
     weighted = grad_one * inputs
     norm_sum_one = jnp.sum(weighted * scale_one, 0)
-    summed = by_batch(after(grad_one.astype(BF16), mlp_own))
-    summed = [queue_scatter_sum(summed[0]), summed[1:].reshape(rows - row_count, full_width)]
-    summed[1] = tp_scatter_sum(summed[1].astype(F32), *project_sent)
-    summed = jnp.concatenate([block.astype(F32) for block in summed])
+    summed = queue_scatter_sum(after(grad_one.astype(BF16), mlp_own)).astype(F32)
     small = jnp.concatenate([norm_sum_one, jnp.sum(weighted * gain_one, -1) / full_width])
     for bit in range((lax.axis_size("tp") - 1).bit_length()):
         small = small + exchange(small, "tp", 1 << bit)
@@ -382,15 +379,15 @@
         - tokens_own.astype(F32) * (scale_one * scale_one * scale_one) * row_mean
     )
     middle_order = owner_order(after(middle_low, *project_sent))
-    out_terms, _ = owner_terms(middle_order, lambda block: dot_tn(heads_out, block), 1)
+    out_terms, out_sent = owner_terms(middle_order, lambda block: dot_tn(heads_out, block), 1)
     grad_scale = (batch_count * row_count * lax.axis_size("fsdp")) ** (-0.5)
     norm_start = lax.axis_index("fsdp") * shard_rows
     norm_sums = norm_sums * grad_scale
-    down_sum = owner_total(down_terms, *project_sent)
-    gate_sum = owner_total(gate_terms, *project_sent)
-    up_sum = owner_total(up_terms, *project_sent)
+    down_sum = owner_total(down_terms, *out_sent)
+    gate_sum = owner_total(gate_terms, *out_sent)
+    up_sum = owner_total(up_terms, *out_sent)
     out_sum = owner_total(out_terms)
-    project_sum = owner_total(project_terms) * grad_scale
+    project_sum = owner_total(project_terms, *out_sent) * grad_scale
     return (
         by_batch(output),
         by_batch(input_grad),

time: 625 us -> 591 us (0.946)
  waiting for transfers between devices: 306 us -> 270 us
  other arithmetic: 61.5 us -> 55 us
    ppermute x31 -> x29, waiting for transfers between devices: 188 us -> 166 us  [exchange(): lax.ppermute(block, axis, [(i, i ^ mask) for i in range(lax.axis_size(axi...]
    reduce_scatter x3, waiting for transfers between devices: 24.3 us -> 10.3 us  [queue_scatter_sum(): lax.psum_scatter(partial.astype(BF16), 'tp', scatter_dimension=1, tiled=T...]
    ppermute x31 -> x29, starting transfers between devices: 27.9 us -> 31.4 us  [exchange(): lax.ppermute(block, axis, [(i, i ^ mask) for i in range(lax.axis_size(axi...]
    unnamed x190 -> x178, local copies, waits for them, and re-layouts: 17.1 us -> 16.4 us
  transfers between devices with their start and end apart: 59 -> 57, of which waited for: 28 -> 25; matrix products, arithmetic and copies ran while one was open for 31% -> 33% of each run, Pallas kernels for 0% -> 0%
where the time goes in v3:
time: 591 us; the launch traced here: 582 us
  waiting for transfers between devices  270 us (46%)
  matrix products  131 us (22%)
  starting transfers between devices  67 us (11%)
  other arithmetic  55 us (9%)
  local copies, waits for them, and re-layouts  43 us (7%)
  between operations  16 us (3%)
    ppermute x29, waiting for transfers between devices, exchange(): lax.ppermute(block, axis, [(i, i ^ mask) for i in range(lax.axis_size(axi...  166 us
    ppermute x6, waiting for transfers between devices, tp_gather(): lax.ppermute(upper, 'tp', [(i, i - 1) for i in range(1, size - step + 1)])  46.9 us
    dot_general x25, matrix products, dot_tn(): lax.dot_general(left, right, (((0,), (0,)), ((), ())), preferred_element_...  42.1 us
    dot_general x5, matrix products, dot_nn(): return jnp.dot(left, right, preferred_element_type=F32)  33.9 us
    ppermute x29, starting transfers between devices, exchange(): lax.ppermute(block, axis, [(i, i ^ mask) for i in range(lax.axis_size(axi...  31.4 us
    all_gather x1, waiting for transfers between devices, queue_gather(): return lax.all_gather(part, 'tp', axis=1, tiled=True)  19 us
    unnamed x178, local copies, waits for them, and re-layouts  16.4 us
    ppermute x8, starting transfers between devices, passed_along(): return lax.ppermute(block, axis, route)  16.4 us
  transfers between devices with their start and end apart: 57, of which 25 were waited for; matrix products, arithmetic and copies ran while one was open for 33% of the time, Pallas kernels for 0%

profile of v3, /device:TPU:0, one launch (start us, length us, event | category | flops | bytes accessed | tf_op | source)
XLA Modules:
  0.0 582.5 jit_solution(16692539099318221672)
XLA Ops:
  12.5 5.8 collective-permute-start
  23.5 5.4 collective-permute-done
  35.8 11.7 %all-gather.6.cloned.1.call-done = bf16[2048,768]{1,0:T(8,128)(2,1)} async-done(((bf16[256,768]{1,0:T(8,128)(2,1)}), bf16[2048,768]{1,0:T(8,128)(2,1)}) %all-gather.6.cloned.1.call-update) | async-done | bytes 3145744 | tf_op jit(solution)/shard_map/all_gather | solution.py:248
  52.7 13.5 %collective-permute-done.5 = bf16[512,512]{1,0:T(8,128)(2,1)} collective-permute-done((bf16[512,512]{1,0:T(8,128)(2,1)S(1)}, bf16[512,512]{1,0:T(8,128)(2,1)}, u32[]{:S(2)}, u32[]{:S(2)}) %collective-permute-start.5) | collective-permute-done | bytes 524320 | tf_op jit(solution)/shard_map/ppermute | solution.py:75
  107.9 10.0 %collective-permute-done.10 = bf16[1,512,512]{2,1,0:T(8,128)(2,1)} collective-permute-done((bf16[1,512,512]{2,1,0:T(8,128)(2,1)S(1)}, bf16[1,512,512]{2,1,0:T(8,128)(2,1)}, u32[]{:S(2)}, u32[]{:S(2)}) %collective-permute-start.10) | collective-permute-done | bytes 524320 | tf_op jit(solution)/shard_map/ppermute | solution.py:57
  125.4 19.0 %collective-permute-done.11 = bf16[2,512,512]{2,1,0:T(8,128)(2,1)} collective-permute-done((bf16[2,512,512]{2,1,0:T(8,128)(2,1)S(1)}, bf16[2,512,512]{2,1,0:T(8,128)(2,1)}, u32[]{:S(2)}, u32[]{:S(2)}) %collective-permute-start.11) | collective-permute-done | bytes 1048608 | tf_op jit(solution)/shard_map/ppermute | solution.py:57
  151.4 23.8 %collective-permute-done.12 = bf16[2,512,512]{2,1,0:T(8,128)(2,1)S(1)} collective-permute-done((bf16[2,512,512]{2,1,0:T(8,128)(2,1)S(1)}, bf16[2,512,512]{2,1,0:T(8,128)(2,1)S(1)}, u32[]{:S(2)}, u32[]{:S(2)}) %collective-permute-start.12) | collective-permute-done | bytes 1048608 | tf_op jit(solution)/shard_map/ppermute | solution.py:57
  176.6 23.6 %collective-permute-done.13 = bf16[1,512,512]{2,1,0:T(8,128)(2,1)S(1)} collective-permute-done((bf16[1,512,512]{2,1,0:T(8,128)(2,1)S(1)}, bf16[1,512,512]{2,1,0:T(8,128)(2,1)S(1)}, u32[]{:S(2)}, u32[]{:S(2)}) %collective-permute-start.13) | collective-permute-done | bytes 524320 | tf_op jit(solution)/shard_map/ppermute | solution.py:57
  204.5 9.9 %collective-permute-done.14 = bf16[512,512]{1,0:T(8,128)(2,1)S(1)} collective-permute-done((bf16[512,512]{1,0:T(8,128)(2,1)S(1)}, bf16[512,512]{1,0:T(8,128)(2,1)S(1)}, u32[]{:S(2)}, u32[]{:S(2)}) %collective-permute-start.14) | collective-permute-done | bytes 524320 | tf_op jit(solution)/shard_map/ppermute | solution.py:74
  220.5 12.4 %collective-permute-done.18 = bf16[512,512]{1,0:T(8,128)(2,1)S(1)} collective-permute-done((bf16[512,512]{1,0:T(8,128)(2,1)S(1)}, bf16[512,512]{1,0:T(8,128)(2,1)S(1)}, u32[]{:S(2)}, u32[]{:S(2)}) %collective-permute-start.18) | collective-permute-done | bytes 524320 | tf_op jit(solution)/shard_map/ppermute | solution.py:75
  235.3 11.4 %collective-permute-done.19 = bf16[512,512]{1,0:T(8,128)(2,1)} collective-permute-done((bf16[512,512]{1,0:T(8,128)(2,1)S(1)}, bf16[512,512]{1,0:T(8,128)(2,1)}, u32[]{:S(2)}, u32[]{:S(2)}) %collective-permute-start.19) | collective-permute-done | bytes 524320 | tf_op jit(solution)/shard_map/ppermute | solution.py:75
  252.6 12.5 %fusion.75 = f32[512,2816]{1,0:T(8,128)} fusion(bf16[512,2048]{1,0:T(8,128)(2,1)} %copy-done.14, bf16[2048,2816]{1,0:T(8,128)(2,1)} %all-gather.10.cloned.1.call-done), kind=kOutput, calls=%fused_computation.251 | convolution fusion | flops 5905580032 | bytes 19398656 | tf_op jit(solution)/shard_map/dot_general | solution.py:45
  265.2 9.5 %multiply_convert_fusion.1 = (bf16[512,1408]{1,0:T(8,128)(2,1)S(1)}, bf16[512,1408]{1,0:T(8,128)(2,1)S(1)}, bf16[512,1408]{1,0:T(8,128)(2,1)S(1)}) fusion(f32[512,2816]{1,0:T(8,128)} %fusion.75, bf16[1408,2048]{1,0:T(8,128)(2,1)} %all-gather.12.cloned.1.call-done, bf16[512,512]{1,0:T(8,128)(2,1)} %copy-done.38, bf16[512,512]{1,0:T(8,128)(2,1)} %copy-done.39, ...), kind=kOutput, calls=%fused_computation.48 | convolution fusion | flops 2972712960 | bytes 17956864 | tf_op jit(solution)/shard_map/dot_general | solution.py:45
  313.2 10.3 %reduce-scatter.4.cloned.1.call-done = bf16[512,512]{1,0:T(8,128)(2,1)} async-done(((bf16[512,2048]{1,0:T(8,128)(2,1)}), bf16[512,512]{1,0:T(8,128)(2,1)}) %reduce-scatter.4.cloned.1.call-update) | async-done | bytes 524304 | tf_op jit(solution)/shard_map/reduce_scatter | solution.py:134
  327.8 7.4 %fusion.5 = bf16[2,8,256,1280]{2,3,1,0:T(8,128)(2,1)} fusion(f32[2,8,256]{2,1,0:T(8,128)S(1)} %log_add_fusion, pred[2,256,1280]{1,2,0:T(8,128)(4,1)S(1)} %bitcast.244, bf16[2,256,8,64]{1,0,3,2:T(2,128)(2,1)S(1)} %copy-done.33, bf16[2,1280,128]{1,2,0:T(8,128)(2,1)S(1)} %copy-done.61), kind=kOutput, calls=%fused_computation.7 | convolution fusion | flops 692060160 | bytes 12009472 | tf_op jit(solution)/shard_map/blhd,bmd->bhlm/dot_general | solution.py:194
  343.6 7.3 %convolution_convert_fusion.3 = bf16[512,2048]{1,0:T(8,128)(2,1)} fusion(bf16[512,1408]{1,0:T(8,128)(2,1)S(1)} %get-tuple-element.167, bf16[1408,2048]{1,0:T(8,128)(2,1)} %all-gather.12.cloned.1.call-done), kind=kOutput, calls=%fused_computation.46 | convolution fusion | flops 2953838592 | bytes 9306112 | tf_op jit(solution)/shard_map/dot_general | solution.py:45
  350.9 19.0 %all-gather.14.cloned.1.call-done = bf16[512,2048]{1,0:T(8,128)(2,1)} async-done(((bf16[512,512]{1,0:T(8,128)(2,1)}), bf16[512,2048]{1,0:T(8,128)(2,1)}) %all-gather.14.cloned.1.call-update) | async-done | bytes 2097168 | tf_op jit(solution)/shard_map/all_gather | solution.py:130
  384.4 8.1 %convolution_bitcast_fusion = f32[2,1280,64]{1,2,0:T(8,128)} fusion(bf16[2,8,256,1280]{2,3,1,0:T(8,128)(2,1)} %fusion.5, bf16[2,256,8,64]{1,3,2,0:T(8,128)(2,1)S(1)} %copy.57), kind=kOutput, calls=%fused_computation.53 | convolution fusion | flops 671088640 | bytes 11665408 | tf_op jit(solution)/shard_map/bhlm,blhd->bmd/dot_general | solution.py:203
  392.5 6.2 %fusion.2 = bf16[2,8,256,1280]{2,3,1,0:T(8,128)(2,1)S(1)} fusion(bf16[2,8,256,1280]{2,3,1,0:T(8,128)(2,1)} %fusion.5, bf16[2,256,8,64]{1,3,2,0:T(8,128)(2,1)S(1)} %copy.57, f32[2,8,256]{2,1,0:T(8,128)S(1)} %bitcast.261, bf16[2,1280,128]{1,2,0:T(8,128)(2,1)} %copy-done.60), kind=kOutput, calls=%fused_computation.3 | convolution fusion | flops 697303040 | bytes 21839872 | tf_op jit(solution)/shard_map/blhd,bmd->bhlm/dot_general | solution.py:204
  427.4 6.0 %multiply_reduce_fusion.1 = (f32[2048]{0:T(1024)S(1)}, f32[512]{0:T(512)S(1)}, bf16[512,2048]{1,0:T(8,128)(2,1)}) fusion(bf16[512,2048]{1,0:T(8,128)(2,1)} %copy-done.15, f32[512]{0:T(512)S(1)} %copy-done.78, f32[2048]{0:T(1024)S(1)} %get-tuple-element.73, bf16[512,640]{0,1:T(8,128)(2,1)S(1)} %pad_maximum_fusion.12, ...), kind=kOutput, calls=%fused_computation.41 | convolution fusion | flops 1349514752 | bytes 7491584 | tf_op jit(solution)/shard_map/dot_general | solution.py:49
  457.2 9.4 %collective-permute-done.30 = f32[4096]{0:T(1024)S(1)} collective-permute-done((f32[4096]{0:T(1024)S(1)}, f32[4096]{0:T(1024)S(1)}, u32[]{:S(2)}, u32[]{:S(2)}) %collective-permute-start.30) | collective-permute-done | bytes 16416 | tf_op jit(solution)/shard_map/ppermute | solution.py:57
  475.6 6.8 %collective-permute-done.42 = bf16[256,1408]{1,0:T(8,128)(2,1)} collective-permute-done((bf16[256,1408]{1,0:T(8,128)(2,1)}, bf16[256,1408]{1,0:T(8,128)(2,1)}, u32[]{:S(2)}, u32[]{:S(2)}) %collective-permute-start.42) | collective-permute-done | bytes 720928 | tf_op jit(solution)/shard_map/ppermute | solution.py:57
  503.7 21.6 %collective-permute-done.43 = bf16[256,1408]{1,0:T(8,128)(2,1)S(1)} collective-permute-done((bf16[256,1408]{1,0:T(8,128)(2,1)}, bf16[256,1408]{1,0:T(8,128)(2,1)S(1)}, u32[]{:S(2)}, u32[]{:S(2)}) %collective-permute-start.43) | collective-permute-done | bytes 720928 | tf_op jit(solution)/shard_map/ppermute | solution.py:57
  529.9 31.0 %collective-permute-done.47 = bf16[1408,256]{1,0:T(8,128)(2,1)S(1)} collective-permute-done((bf16[1408,256]{1,0:T(8,128)(2,1)}, bf16[1408,256]{1,0:T(8,128)(2,1)S(1)}, u32[]{:S(2)}, u32[]{:S(2)}) %collective-permute-start.47) | collective-permute-done | bytes 720928 | tf_op jit(solution)/shard_map/ppermute | solution.py:57
  (421 shorter events, 264.9 us)
Async XLA Ops:
  7.2 40.3 %all-gather.6.cloned.1.call-start = ((), (), s32[]{:S(2)}) async-start(), calls=%async_computation.3 | async-start | bytes 3538944 | tf_op jit(solution)/shard_map/all_gather | solution.py:248
  12.4 135.3 %all-gather.8.cloned.1.call-start = ((), (), s32[]{:S(2)}) async-start(), calls=%async_computation.4 | async-start | bytes 2359296 | tf_op jit(solution)/shard_map/all_gather | solution.py:264
  69.1 183.5 %all-gather.10.cloned.1.call-start = ((), (), s32[]{:S(2)}) async-start(), calls=%async_computation.5 | async-start | bytes 12976128 | tf_op jit(solution)/shard_map/all_gather | solution.py:265
  69.9 195.3 %all-gather.12.cloned.1.call-start = ((), (), s32[]{:S(2)}) async-start(), calls=%async_computation.6 | async-start | bytes 6488064 | tf_op jit(solution)/shard_map/all_gather | solution.py:268
  92.6 25.3 %collective-permute-start.10 = (bf16[1,512,512]{2,1,0:T(8,128)(2,1)S(1)}, bf16[1,512,512]{2,1,0:T(8,128)(2,1)}, u32[]{:S(2)}, u32[]{:S(2)}) collective-permute-start(bf16[1,512,512]{2,1,0:T(8,128)(2,1)S(1)} %bitcast.257), channel_id=1, source_target_pairs={{0,2},{1,3},{2,0},{3,1},{4,6},{5,7},{6,4},{7,5},{8,10},{9,11},{10,... | collective-permute-start | bytes 1572872 | tf_op jit(solution)/shard_map/ppermute | solution.py:57
  93.1 230.4 %reduce-scatter.4.cloned.1.call-start = ((), (), s32[]{:S(2)}) async-start(), calls=%async_computation.7 | async-start | bytes 2621440 | tf_op jit(solution)/shard_map/reduce_scatter | solution.py:134
  119.1 25.3 %collective-permute-start.11 = (bf16[2,512,512]{2,1,0:T(8,128)(2,1)S(1)}, bf16[2,512,512]{2,1,0:T(8,128)(2,1)}, u32[]{:S(2)}, u32[]{:S(2)}) collective-permute-start(bf16[2,512,512]{2,1,0:T(8,128)(2,1)S(1)} %pad_maximum_fusion.5), channel_id=1, source_target_pairs={{0,1},{1,0},{2,3},{3,2},{4,5},{5,4},{6,7},{7,6},{8,9},{9,8},{10,11... | collective-permute-start | bytes 3145736 | tf_op jit(solution)/shard_map/ppermute | solution.py:57
  282.9 86.9 %all-gather.14.cloned.1.call-start = ((), (), s32[]{:S(2)}) async-start(), calls=%async_computation.8 | async-start | bytes 2621440 | tf_op jit(solution)/shard_map/all_gather | solution.py:130
  323.5 147.5 %reduce-scatter.6.cloned.1.call-start = ((), (), s32[]{:S(2)}) async-start(), calls=%async_computation.9 | async-start | bytes 2621440 | tf_op jit(solution)/shard_map/reduce_scatter | solution.py:134
  338.5 116.7 %collective-permute-start.45 = (bf16[1408,1024]{1,0:T(8,128)(2,1)}, bf16[1408,1024]{1,0:T(8,128)(2,1)}, u32[]{:S(2)}, u32[]{:S(2)}) collective-permute-start(bf16[1408,1024]{1,0:T(8,128)(2,1)} %convolution_convert_fusion), channel_id=1, source_target_pairs={{0,4},{4,0},{8,12},{12,8},{16,20},{20,16},{24,28},{28,24},{1,5},{5... | collective-permute-start | bytes 8650760 | tf_op jit(solution)/shard_map/ppermute | solution.py:57
  407.8 164.9 %reduce-scatter.8.cloned.1.call-start = ((), (), s32[]{:S(2)}) async-start(), calls=%async_computation.10 | async-start | bytes 2621440 | tf_op jit(solution)/shard_map/reduce_scatter | solution.py:134
  417.9 53.1 %collective-permute-start.39 = (bf16[256,1408]{1,0:T(8,128)(2,1)}, bf16[256,1408]{1,0:T(8,128)(2,1)}, u32[]{:S(2)}, u32[]{:S(2)}) collective-permute-start(bf16[256,1408]{1,0:T(8,128)(2,1)} %get-tuple-element.182), channel_id=1, source_target_pairs={{0,8},{4,12},{8,0},{12,4},{16,24},{20,28},{24,16},{28,20},{1,9},{5... | collective-permute-start | bytes 2162696 | tf_op jit(solution)/shard_map/ppermute | solution.py:57
  421.3 50.8 %collective-permute-start.40 = (bf16[256,1408]{1,0:T(8,128)(2,1)}, bf16[256,1408]{1,0:T(8,128)(2,1)}, u32[]{:S(2)}, u32[]{:S(2)}) collective-permute-start(bf16[256,1408]{1,0:T(8,128)(2,1)} %get-tuple-element.181), channel_id=1, source_target_pairs={{0,16},{4,20},{8,24},{12,28},{16,0},{20,4},{24,8},{28,12},{1,17},{... | collective-permute-start | bytes 2162696 | tf_op jit(solution)/shard_map/ppermute | solution.py:57
  455.2 27.2 %collective-permute-start.42 = (bf16[256,1408]{1,0:T(8,128)(2,1)}, bf16[256,1408]{1,0:T(8,128)(2,1)}, u32[]{:S(2)}, u32[]{:S(2)}) collective-permute-start(bf16[256,1408]{1,0:T(8,128)(2,1)} %get-tuple-element.178), channel_id=1, source_target_pairs={{0,8},{4,12},{8,0},{12,4},{16,24},{20,28},{24,16},{28,20},{1,9},{5... | collective-permute-start | bytes 2162696 | tf_op jit(solution)/shard_map/ppermute | solution.py:57
  466.7 32.4 %collective-permute-start.35 = (bf16[512,1024]{1,0:T(8,128)(2,1)}, bf16[512,1024]{1,0:T(8,128)(2,1)}, u32[]{:S(2)}, u32[]{:S(2)}) collective-permute-start(bf16[512,1024]{1,0:T(8,128)(2,1)} %convolution_convert_fusion.5), channel_id=1, source_target_pairs={{0,4},{4,0},{8,12},{12,8},{16,20},{20,16},{24,28},{28,24},{1,5},{5... | collective-permute-start | bytes 3145736 | tf_op jit(solution)/shard_map/ppermute | solution.py:57
  472.7 26.4 %collective-permute-start.34 = (bf16[256,640]{1,0:T(8,128)(2,1)S(1)}, bf16[256,640]{1,0:T(8,128)(2,1)S(1)}, u32[]{:S(2)}, u32[]{:S(2)}) collective-permute-start(bf16[256,640]{1,0:T(8,128)(2,1)S(1)} %copy-done.73), channel_id=1, source_target_pairs={{0,24},{4,28},{8,16},{12,20},{16,8},{20,12},{24,0},{28,4},{1,25},{... | collective-permute-start | bytes 983048 | tf_op jit(solution)/shard_map/ppermute | solution.py:57
  482.4 42.9 %collective-permute-start.43 = (bf16[256,1408]{1,0:T(8,128)(2,1)}, bf16[256,1408]{1,0:T(8,128)(2,1)S(1)}, u32[]{:S(2)}, u32[]{:S(2)}) collective-permute-start(bf16[256,1408]{1,0:T(8,128)(2,1)} %get-tuple-element.177), channel_id=1, source_target_pairs={{0,16},{4,20},{8,24},{12,28},{16,0},{20,4},{24,8},{28,12},{1,17},{... | collective-permute-start | bytes 2162696 | tf_op jit(solution)/shard_map/ppermute | solution.py:57
  489.3 36.6 %collective-permute-start.44 = (bf16[256,1408]{1,0:T(8,128)(2,1)}, bf16[256,1408]{1,0:T(8,128)(2,1)S(1)}, u32[]{:S(2)}, u32[]{:S(2)}) collective-permute-start(bf16[256,1408]{1,0:T(8,128)(2,1)} %get-tuple-element.176), channel_id=1, source_target_pairs={{0,24},{4,28},{8,16},{12,20},{16,8},{20,12},{24,0},{28,4},{1,25},{... | collective-permute-start | bytes 2162696 | tf_op jit(solution)/shard_map/ppermute | solution.py:57
  492.0 35.3 %collective-permute-start.46 = (bf16[1408,256]{1,0:T(8,128)(2,1)}, bf16[1408,256]{1,0:T(8,128)(2,1)S(1)}, u32[]{:S(2)}, u32[]{:S(2)}) collective-permute-start(bf16[1408,256]{1,0:T(8,128)(2,1)} %get-tuple-element.173), channel_id=1, source_target_pairs={{0,8},{4,12},{8,0},{12,4},{16,24},{20,28},{24,16},{28,20},{1,9},{5... | collective-permute-start | bytes 2162696 | tf_op jit(solution)/shard_map/ppermute | solution.py:57
  499.1 61.8 %collective-permute-start.47 = (bf16[1408,256]{1,0:T(8,128)(2,1)}, bf16[1408,256]{1,0:T(8,128)(2,1)S(1)}, u32[]{:S(2)}, u32[]{:S(2)}) collective-permute-start(bf16[1408,256]{1,0:T(8,128)(2,1)} %get-tuple-element.172), channel_id=1, source_target_pairs={{0,16},{4,20},{8,24},{12,28},{16,0},{20,4},{24,8},{28,12},{1,17},{... | collective-permute-start | bytes 2162696 | tf_op jit(solution)/shard_map/ppermute | solution.py:57
  499.1 61.8 %collective-permute-start.48 = (bf16[1408,256]{1,0:T(8,128)(2,1)}, bf16[1408,256]{1,0:T(8,128)(2,1)S(1)}, u32[]{:S(2)}, u32[]{:S(2)}) collective-permute-start(bf16[1408,256]{1,0:T(8,128)(2,1)} %get-tuple-element.171), channel_id=1, source_target_pairs={{0,24},{4,28},{8,16},{12,20},{16,8},{20,12},{24,0},{28,4},{1,25},{... | collective-permute-start | bytes 2162696 | tf_op jit(solution)/shard_map/ppermute | solution.py:57
  525.3 45.5 %collective-permute-start.36 = (bf16[512,256]{1,0:T(8,128)(2,1)}, bf16[512,256]{1,0:T(8,128)(2,1)S(1)}, u32[]{:S(2)}, u32[]{:S(2)}) collective-permute-start(bf16[512,256]{1,0:T(8,128)(2,1)} %get-tuple-element.234), channel_id=1, source_target_pairs={{0,8},{4,12},{8,0},{12,4},{16,24},{20,28},{24,16},{28,20},{1,9},{5... | collective-permute-start | bytes 786440 | tf_op jit(solution)/shard_map/ppermute | solution.py:57
  525.9 44.9 %collective-permute-start.37 = (bf16[512,256]{1,0:T(8,128)(2,1)}, bf16[512,256]{1,0:T(8,128)(2,1)S(1)}, u32[]{:S(2)}, u32[]{:S(2)}) collective-permute-start(bf16[512,256]{1,0:T(8,128)(2,1)} %get-tuple-element.233), channel_id=1, source_target_pairs={{0,16},{4,20},{8,24},{12,28},{16,0},{20,4},{24,8},{28,12},{1,17},{... | collective-permute-start | bytes 786440 | tf_op jit(solution)/shard_map/ppermute | solution.py:57
  527.3 43.5 %collective-permute-start.38 = (bf16[512,256]{1,0:T(8,128)(2,1)}, bf16[512,256]{1,0:T(8,128)(2,1)S(1)}, u32[]{:S(2)}, u32[]{:S(2)}) collective-permute-start(bf16[512,256]{1,0:T(8,128)(2,1)} %get-tuple-element.232), channel_id=1, source_target_pairs={{0,24},{4,28},{8,16},{12,20},{16,8},{20,12},{24,0},{28,4},{1,25},{... | collective-permute-start | bytes 786440 | tf_op jit(solution)/shard_map/ppermute | solution.py:57
  (117 other events, 1220.2 us)
Sparse Core Ops, SparseCore 0:
  12.5 34.9 all-gather.5
  69.2 31.8 all-gather.7
  103.6 67.5 all-gather.9
  173.0 44.2 all-gather.11
  283.0 40.4 reduce-scatter.3
  324.9 44.8 all-gather.13
  407.9 42.9 reduce-scatter.5
  471.2 41.9 reduce-scatter.7
